TPU v7x, 256 devices: a whole 4x4x8 slice. The times are simulated.
256 devices in a mesh: step: 64 (over z, y, core), space: 4 (over x).
Axes of the slice: x: 4, y: 4, z: 8, core: 2. Of those that a mesh axis runs over, the one named last changes fastest.
Arguments:
- guesses: float32 [64, 64, 4, 2560], P('step', None, None, 'space'), may hold values from -6 to 6
- noise: float32 [64, 64, 4, 2560], P('step', None, None, 'space'), may hold values from -6 to 6
- timesteps: int32 [64, 2], P('step'), may hold values from 1 to 999, as said below
- conv_first: bfloat16 [3, 256, 576], replicated, may hold values from -0.15625 to 0.15625
- conv_second: bfloat16 [3, 64, 2304], replicated, may hold values from -0.078125 to 0.078125
- time_weight: float32 [64, 256], replicated, may hold values from -0.75 to 0.75
Outputs:
- states: float32 [64, 64, 4, 2560], P('step', None, None, 'space')
- changes: float32 [64], P('step')
Inputs may be any that keep to these rules, and one draw needn't show every extreme that they name: Row k holds the timesteps before and after step k: the first entry of row 0 is 999, the second entry of the last row is 1, each row's second entry equals the next row's first, and the first entries fall strictly.
All inputs are finite; a program needn't handle non-finite values.
Results may differ from a plain program's by a relative error of at most 0.0019.
Values may be sent and summed in bfloat16 or wider, within the bound.
A program may use at most 64 MiB of HBM per device.

v0:
```python
import math

import jax
import jax.numpy as jnp
from jax import lax
from jax.sharding import PartitionSpec as P

C = 64
COLS = 80


def padded_2(cells, sides, width):
    for axis, dim in sides:
        count = lax.axis_size(axis)
        ends = count - 1
        head = lax.slice_in_dim(cells, 0, width, axis=dim)
        tail = lax.slice_in_dim(cells, cells.shape[dim] - width, cells.shape[dim], axis=dim)
        cells = jnp.concatenate(
            [
                lax.ppermute(tail, axis, [(i, (i + 1) % count) for i in range(ends)]),
                cells,
                lax.ppermute(head, axis, [((i + 1) % count, i) for i in range(ends)]),
            ],
            axis=dim,
        )
    return cells


def plan(timestep):
    scaled = timestep.astype(jnp.float32) / 1000.0
    return -(0.1 * scaled + 9.95 * scaled * scaled)


def coefficients(timestep_pair):
    log_from = plan(timestep_pair[0])
    log_to = plan(timestep_pair[1])
    half_gap = 0.5 * (log_to - log_from)
    decay_gain = jnp.expm1(half_gap)
    remain_from = -jnp.expm1(log_from)
    remain_to = -jnp.expm1(log_to)
    ratio_term = -jnp.expm1(log_from - log_to)
    noise_gain = -jnp.exp(half_gap) * jnp.sqrt(remain_from) + remain_to * jnp.exp(
        -half_gap
    ) / jnp.sqrt(remain_from)
    spread_gain = jnp.sqrt(remain_to / remain_from * ratio_term)
    return (decay_gain, noise_gain, spread_gain)


def time_embed(timestep, time_weight):
    half_count = C // 2
    frequency = jnp.exp(-math.log(10000.0) * jnp.arange(half_count, dtype=jnp.float32) / half_count)
    angles = timestep.astype(jnp.float32) * frequency
    features = jnp.concatenate([jnp.sin(angles), jnp.cos(angles)])
    return jnp.dot(
        features, time_weight, preferred_element_type=jnp.float32, precision=lax.Precision.HIGHEST
    )


def convolve(padded, weight, rows_out):
    length = rows_out * COLS
    extended = jnp.pad(padded, ((0, 0), (0, 0), (1, 1)))
    column = jnp.arange(length) % COLS
    zero_value = jnp.zeros((), padded.dtype)
    pieces = []
    for row_shift in range(3):
        for col_shift in range(3):
            offset_start = 1 + row_shift * COLS + col_shift - 1
            window_piece = extended[:, :, offset_start : offset_start + length]
            if col_shift == 0:
                window_piece = jnp.where(column >= 1, window_piece, zero_value)
            if col_shift == 2:
                window_piece = jnp.where(column <= COLS - 2, window_piece, zero_value)
            pieces.append(window_piece)
    stacked = jnp.concatenate(pieces, axis=0)
    framed = jnp.pad(stacked, ((0, 0), (1, 1), (0, 0)))
    frame_count = padded.shape[1]
    result = jnp.einsum(
        "oj,jfp->ofp", weight[0], framed[:, 0:frame_count], preferred_element_type=jnp.float32
    )
    for frame_shift in range(1, 3):
        result = result + jnp.einsum(
            "oj,jfp->ofp",
            weight[frame_shift],
            framed[:, frame_shift : frame_shift + frame_count],
            preferred_element_type=jnp.float32,
        )
    return result


def earlier_total(column_block):
    step_count = column_block.shape[0]
    later_index = jnp.arange(step_count)[:, None]
    earlier_index = jnp.arange(step_count)[None, :]
    lower_table = (earlier_index < later_index).astype(jnp.float32)
    return jnp.einsum("kj,j...->k...", lower_table, column_block, precision=lax.Precision.HIGHEST)


def local(guesses, noise, timesteps, conv_first, conv_second, time_weight):
    step_index = lax.axis_index("step")
    space_count = lax.axis_size("space")
    start_latent = guesses[0]
    noise_step = noise[0]
    timestep_pair = timesteps[0]
    decay_gain, noise_gain, spread_gain = coefficients(timestep_pair)
    temb = time_embed(timestep_pair[0], time_weight)
    row_count = start_latent.shape[2] // COLS
    is_anchor = step_index == 0

    def denoise(latent):
        rounded = latent.astype(jnp.bfloat16)
        padded = padded_2(rounded, (("space", 2),), COLS)
        hidden = jax.nn.silu(convolve(padded, conv_first, row_count) + temb[:, None, None]).astype(
            jnp.bfloat16
        )
        hidden_padded = padded_2(hidden, (("space", 2),), COLS)
        return convolve(hidden_padded, conv_second, row_count)

    def prefix(scan_term):
        before_sum = earlier_total(
            lax.all_to_all(scan_term[None], "step", split_axis=1, concat_axis=0, tiled=True)
        )
        return lax.all_to_all(before_sum, "step", split_axis=0, concat_axis=1, tiled=True)[0]

    def picard_sweep(latent):
        drift = decay_gain * latent + noise_gain * denoise(latent) + spread_gain * noise_step
        scan_term = drift + jnp.where(is_anchor, latent, 0.0)
        before_sum = prefix(scan_term)
        advanced = jnp.where(is_anchor, latent, before_sum)
        return (advanced, advanced + drift)

    entering_one, reached_one = picard_sweep(start_latent)
    entering_two, reached_two = picard_sweep(entering_one)
    difference = reached_two - reached_one
    local_sum = jnp.sum(difference * difference)
    norm_total = lax.psum(local_sum, "space")
    cell_count = difference.shape[0] * difference.shape[1] * difference.shape[2] * space_count
    changes = jnp.sqrt(norm_total / cell_count).reshape(1)
    return (reached_two[None], changes)


def solution(mesh):
    in_specs = (
        P("step", None, None, "space"),
        P("step", None, None, "space"),
        P("step", None),
        P(),
        P(),
        P(),
    )
    out_specs = (P("step", None, None, "space"), P("step"))
    return jax.shard_map(local, mesh=mesh, in_specs=in_specs, out_specs=out_specs, check_vma=False)
```

profile of v0, /device:TPU:1, one launch (start us, length us, event | category | flops | bytes accessed | tf_op | source)
XLA Modules:
  0.0 203.7 jit_solution(4758384853685982510)
XLA Ops:
  1.9 3.9 %collective-permute-start = (bf16[64,4,80]{2,0,1:T(8,128)(2,1)S(1)}, bf16[64,4,80]{2,0,1:T(8,128)(2,1)S(1)}, u32[]{:S(2)}, u32[]{:S(2)}) collective-permute-start(bf16[64,4,80]{2,0,1:T(8,128)(2,1)S(1)} %get-tuple-element.16), channel_id=1, source_target_pairs={{0,1},{1,2},{2,3},{4,5},{5,6},{6,7},{8,9},{9,10},{10,11},{12,13},{... | collective-permute-start | bytes 122888 | tf_op jit(solution)/shard_map/ppermute | solution.py:20
  7.2 1.3 fusion.145
  9.5 1.4 collective-permute-done.1
  15.2 1.5 fusion.7
  16.8 3.1 %collective-permute-start.2 = (bf16[256,4,80]{0,2,1:T(8,128)(2,1)S(1)}, bf16[256,4,80]{0,2,1:T(8,128)(2,1)S(1)}, u32[]{:S(2)}, u32[]{:S(2)}) collective-permute-start(bf16[256,4,80]{0,2,1:T(8,128)(2,1)S(1)} %get-tuple-element.12), channel_id=1, source_target_pairs={{0,1},{1,2},{2,3},{4,5},{5,6},{6,7},{8,9},{9,10},{10,11},{12,13},{... | collective-permute-start | bytes 491528 | tf_op jit(solution)/shard_map/ppermute | solution.py:20
  19.9 1.5 collective-permute-start.3
  22.5 3.5 %collective-permute-done.3 = bf16[256,4,80]{0,2,1:T(8,128)(2,1)S(1)} collective-permute-done((bf16[256,4,80]{0,2,1:T(8,128)(2,1)S(1)}, bf16[256,4,80]{0,2,1:T(8,128)(2,1)S(1)}, u32[]{:S(2)}, u32[]{:S(2)}) %collective-permute-start.3) | collective-permute-done | bytes 163872 | tf_op jit(solution)/shard_map/ppermute | solution.py:22
  29.8 3.6 %fusion.99 = f32[4,640,64]{1,2,0:T(8,128)S(1)} fusion(bf16[2304,4,640]{0,2,1:T(8,128)(2,1)S(1)} %fusion.37, bf16[3,64,2304]{2,1,0:T(8,128)(2,1)S(1)} %copy-done.2), kind=kOutput, calls=%fused_computation.175 | convolution fusion | flops 754974720 | bytes 12746752 | tf_op jit(solution)/shard_map/oj,jfp->ofp/dot_general | solution.py:81
  33.4 2.9 %fusion.95 = f32[4,640,64]{1,2,0:T(8,128)S(1)} fusion(bf16[2304,4,640]{0,2,1:T(8,128)(2,1)S(1)} %fusion.37, bf16[3,64,2304]{2,1,0:T(8,128)(2,1)S(1)} %copy-done.2), kind=kOutput, calls=%fused_computation.171 | convolution fusion | flops 566231040 | bytes 12746752 | tf_op jit(solution)/shard_map/oj,jfp->ofp/dot_general | solution.py:81
  36.3 3.1 %fusion.50 = f32[64,4,640]{2,0,1:T(8,128)S(1)} fusion(f32[4,640,64]{1,2,0:T(8,128)S(1)} %fusion.95, f32[4,640,64]{1,2,0:T(8,128)S(1)} %fusion.99, bf16[2304,4,640]{0,2,1:T(8,128)(2,1)S(1)} %fusion.37, f32[1,64,4,640]{3,2,1,0:T(4,128)S(1)} %copy-done.5, f32[1,64,4,640]{3,2,1,0:T(4,128)S(1)} %copy-done.1, f32[]{:T(128)S(6)} %sqrt.11, f32[]{:T(128)S(6)} %add.174, ...), kind=kOutput, calls=%fused_computation.90 | convolution fusion | flops 567377920 | bytes 15368204 | tf_op jit(solution)/shard_map/oj,jfp->ofp/dot_general | solution.py:77
  40.0 35.3 %all_to_all.16 = f32[1,64,4,640]{3,2,0,1:T(4,128)S(1)} all-to-all(f32[1,64,4,640]{3,2,0,1:T(4,128)S(1)} %copy.22), channel_id=1, replica_groups=mesh['step'=64,'space'=4] {'step'}, dimensions={1} | all-to-all | bytes 1310720 | tf_op jit(solution)/shard_map/all_to_all | solution.py:120
  76.2 25.9 %all_to_all.17 = f32[64,1,4,640]{3,2,1,0:T(4,128)S(1)} all-to-all(f32[64,1,4,640]{3,2,1,0:T(4,128)S(1)} %copy.24), channel_id=1, replica_groups=mesh['step'=64,'space'=4] {'step'}, dimensions={0} | all-to-all | bytes 1310720 | tf_op jit(solution)/shard_map/all_to_all | solution.py:122
  102.4 2.8 %collective-permute-start.4 = (bf16[64,4,80]{2,0,1:T(8,128)(2,1)S(1)}, bf16[64,4,80]{2,0,1:T(8,128)(2,1)S(1)}, u32[]{:S(2)}, u32[]{:S(2)}) collective-permute-start(bf16[64,4,80]{2,0,1:T(8,128)(2,1)S(1)} %get-tuple-element.14), channel_id=1, source_target_pairs={{0,1},{1,2},{2,3},{4,5},{5,6},{6,7},{8,9},{9,10},{10,11},{12,13},{... | collective-permute-start | bytes 122888 | tf_op jit(solution)/shard_map/ppermute | solution.py:20
  105.2 1.5 collective-permute-start.5
  106.7 3.5 %collective-permute-done.5 = bf16[64,4,80]{2,0,1:T(8,128)(2,1)S(1)} collective-permute-done((bf16[64,4,80]{2,0,1:T(8,128)(2,1)S(1)}, bf16[64,4,80]{2,0,1:T(8,128)(2,1)S(1)}, u32[]{:S(2)}, u32[]{:S(2)}) %collective-permute-start.5) | collective-permute-done | bytes 40992 | tf_op jit(solution)/shard_map/ppermute | solution.py:22
  114.5 1.5 fusion.8
  116.0 1.9 collective-permute-start.6
  120.2 3.8 %collective-permute-done.7 = bf16[256,4,80]{0,2,1:T(8,128)(2,1)S(1)} collective-permute-done((bf16[256,4,80]{0,2,1:T(8,128)(2,1)S(1)}, bf16[256,4,80]{0,2,1:T(8,128)(2,1)S(1)}, u32[]{:S(2)}, u32[]{:S(2)}) %collective-permute-start.7) | collective-permute-done | bytes 163872 | tf_op jit(solution)/shard_map/ppermute | solution.py:22
  127.2 3.6 %fusion.97 = f32[4,640,64]{1,2,0:T(8,128)S(1)} fusion(bf16[2304,4,640]{0,2,1:T(8,128)(2,1)S(1)} %fusion.32, bf16[3,64,2304]{2,1,0:T(8,128)(2,1)S(1)} %copy-done.2), kind=kOutput, calls=%fused_computation.173 | convolution fusion | flops 754974720 | bytes 12746752 | tf_op jit(solution)/shard_map/oj,jfp->ofp/dot_general | solution.py:81
  130.9 2.9 %fusion.93 = f32[4,640,64]{1,2,0:T(8,128)S(1)} fusion(bf16[2304,4,640]{0,2,1:T(8,128)(2,1)S(1)} %fusion.32, bf16[3,64,2304]{2,1,0:T(8,128)(2,1)S(1)} %copy-done.2), kind=kOutput, calls=%fused_computation.169 | convolution fusion | flops 566231040 | bytes 12746752 | tf_op jit(solution)/shard_map/oj,jfp->ofp/dot_general | solution.py:81
  133.8 3.1 %fusion.51 = f32[64,4,640]{2,0,1:T(8,128)S(1)} fusion(f32[4,640,64]{1,2,0:T(8,128)S(1)} %fusion.93, f32[4,640,64]{1,2,0:T(8,128)S(1)} %fusion.97, bf16[2304,4,640]{0,2,1:T(8,128)(2,1)S(1)} %fusion.32, f32[64,4,640]{2,0,1:T(8,128)S(1)} %get-tuple-element.7, f32[1,64,4,640]{3,2,1,0:T(4,128)S(1)} %copy-done.5, f32[]{:T(128)S(6)} %sqrt.11, f32[]{:T(128)S(6)} %add.174, ...), kind=kOutput, calls=%fused_computation.91 | convolution fusion | flops 567377920 | bytes 15368204 | tf_op jit(solution)/shard_map/oj,jfp->ofp/dot_general | solution.py:77
  137.4 28.6 %all_to_all.18 = f32[1,64,4,640]{3,2,0,1:T(4,128)S(1)} all-to-all(f32[1,64,4,640]{3,2,0,1:T(4,128)S(1)} %copy.29), channel_id=1, replica_groups=mesh['step'=64,'space'=4] {'step'}, dimensions={1} | all-to-all | bytes 1310720 | tf_op jit(solution)/shard_map/all_to_all | solution.py:120
  166.9 25.9 %all_to_all.19 = f32[64,1,4,640]{3,2,1,0:T(4,128)S(1)} all-to-all(f32[64,1,4,640]{3,2,1,0:T(4,128)S(1)} %copy.31), channel_id=1, replica_groups=mesh['step'=64,'space'=4] {'step'}, dimensions={0} | all-to-all | bytes 1310720 | tf_op jit(solution)/shard_map/all_to_all | solution.py:122
  193.7 6.9 %psum.7 = f32[]{:T(128)} all-reduce(f32[]{:T(128)} %get-tuple-element.8), channel_id=1, replica_groups=mesh['step'=64,'space'=4] {'space'}, use_global_device_ids=true, to_apply=%region_1.2 | all-reduce | flops 1 | bytes 8 | tf_op jit(solution)/shard_map/psum | solution.py:135
  (82 shorter events, 25.4 us)
Async XLA Ops:
  0.6 8.6 %copy-start = (f32[64,256]{1,0:T(8,128)S(1)}, f32[64,256]{1,0:T(8,128)}, u32[]{:S(2)}) copy-start(f32[64,256]{1,0:T(8,128)} %param.11) | copy-start | bytes 196612
  0.6 11.2 %copy-start.1 = (f32[1,64,4,640]{3,2,1,0:T(4,128)S(1)}, f32[1,64,4,640]{3,2,1,0:T(4,128)}, u32[]{:S(2)}) copy-start(f32[1,64,4,640]{3,2,1,0:T(4,128)} %param.6) | copy-start | bytes 1966084
  1.9 7.5 %collective-permute-start = (bf16[64,4,80]{2,0,1:T(8,128)(2,1)S(1)}, bf16[64,4,80]{2,0,1:T(8,128)(2,1)S(1)}, u32[]{:S(2)}, u32[]{:S(2)}) collective-permute-start(bf16[64,4,80]{2,0,1:T(8,128)(2,1)S(1)} %get-tuple-element.16), channel_id=1, source_target_pairs={{0,1},{1,2},{2,3},{4,5},{5,6},{6,7},{8,9},{9,10},{10,11},{12,13},{... | collective-permute-start | bytes 122888 | tf_op jit(solution)/shard_map/ppermute | solution.py:20
  5.9 5.0 %collective-permute-start.1 = (bf16[64,4,80]{2,0,1:T(8,128)(2,1)S(1)}, bf16[64,4,80]{2,0,1:T(8,128)(2,1)S(1)}, u32[]{:S(2)}, u32[]{:S(2)}) collective-permute-start(bf16[64,4,80]{2,0,1:T(8,128)(2,1)S(1)} %get-tuple-element.17), channel_id=1, source_target_pairs={{1,0},{2,1},{3,2},{5,4},{6,5},{7,6},{9,8},{10,9},{11,10},{13,12},{... | collective-permute-start | bytes 122888 | tf_op jit(solution)/shard_map/ppermute | solution.py:22
  11.5 1.3 copy-start.3
  16.8 5.7 %collective-permute-start.2 = (bf16[256,4,80]{0,2,1:T(8,128)(2,1)S(1)}, bf16[256,4,80]{0,2,1:T(8,128)(2,1)S(1)}, u32[]{:S(2)}, u32[]{:S(2)}) collective-permute-start(bf16[256,4,80]{0,2,1:T(8,128)(2,1)S(1)} %get-tuple-element.12), channel_id=1, source_target_pairs={{0,1},{1,2},{2,3},{4,5},{5,6},{6,7},{8,9},{9,10},{10,11},{12,13},{... | collective-permute-start | bytes 491528 | tf_op jit(solution)/shard_map/ppermute | solution.py:20
  19.9 6.1 %collective-permute-start.3 = (bf16[256,4,80]{0,2,1:T(8,128)(2,1)S(1)}, bf16[256,4,80]{0,2,1:T(8,128)(2,1)S(1)}, u32[]{:S(2)}, u32[]{:S(2)}) collective-permute-start(bf16[256,4,80]{0,2,1:T(8,128)(2,1)S(1)} %get-tuple-element.13), channel_id=1, source_target_pairs={{1,0},{2,1},{3,2},{5,4},{6,5},{7,6},{9,8},{10,9},{11,10},{13,12},{... | collective-permute-start | bytes 491528 | tf_op jit(solution)/shard_map/ppermute | solution.py:22
  28.6 1.2 copy-start.2
  33.4 2.9 %copy-start.5 = (f32[1,64,4,640]{3,2,1,0:T(4,128)S(1)}, f32[1,64,4,640]{3,2,1,0:T(4,128)}, u32[]{:S(2)}) copy-start(f32[1,64,4,640]{3,2,1,0:T(4,128)} %param.7) | copy-start | bytes 1966084
  102.4 4.4 %collective-permute-start.4 = (bf16[64,4,80]{2,0,1:T(8,128)(2,1)S(1)}, bf16[64,4,80]{2,0,1:T(8,128)(2,1)S(1)}, u32[]{:S(2)}, u32[]{:S(2)}) collective-permute-start(bf16[64,4,80]{2,0,1:T(8,128)(2,1)S(1)} %get-tuple-element.14), channel_id=1, source_target_pairs={{0,1},{1,2},{2,3},{4,5},{5,6},{6,7},{8,9},{9,10},{10,11},{12,13},{... | collective-permute-start | bytes 122888 | tf_op jit(solution)/shard_map/ppermute | solution.py:20
  105.2 5.0 %collective-permute-start.5 = (bf16[64,4,80]{2,0,1:T(8,128)(2,1)S(1)}, bf16[64,4,80]{2,0,1:T(8,128)(2,1)S(1)}, u32[]{:S(2)}, u32[]{:S(2)}) collective-permute-start(bf16[64,4,80]{2,0,1:T(8,128)(2,1)S(1)} %get-tuple-element.15), channel_id=1, source_target_pairs={{1,0},{2,1},{3,2},{5,4},{6,5},{7,6},{9,8},{10,9},{11,10},{13,12},{... | collective-permute-start | bytes 122888 | tf_op jit(solution)/shard_map/ppermute | solution.py:22
  110.8 1.2 copy-start.4
  116.0 4.2 %collective-permute-start.6 = (bf16[256,4,80]{0,2,1:T(8,128)(2,1)S(1)}, bf16[256,4,80]{0,2,1:T(8,128)(2,1)S(1)}, u32[]{:S(2)}, u32[]{:S(2)}) collective-permute-start(bf16[256,4,80]{0,2,1:T(8,128)(2,1)S(1)} %get-tuple-element.10), channel_id=1, source_target_pairs={{0,1},{1,2},{2,3},{4,5},{5,6},{6,7},{8,9},{9,10},{10,11},{12,13},{... | collective-permute-start | bytes 491528 | tf_op jit(solution)/shard_map/ppermute | solution.py:20
  118.0 6.1 %collective-permute-start.7 = (bf16[256,4,80]{0,2,1:T(8,128)(2,1)S(1)}, bf16[256,4,80]{0,2,1:T(8,128)(2,1)S(1)}, u32[]{:S(2)}, u32[]{:S(2)}) collective-permute-start(bf16[256,4,80]{0,2,1:T(8,128)(2,1)S(1)} %get-tuple-element.11), channel_id=1, source_target_pairs={{1,0},{2,1},{3,2},{5,4},{6,5},{7,6},{9,8},{10,9},{11,10},{13,12},{... | collective-permute-start | bytes 491528 | tf_op jit(solution)/shard_map/ppermute | solution.py:22
where the time goes:
time: 205 us; the launch traced here: 204 us
  blocking collectives  123 us (60%)
  matrix products  28.4 us (14%)
  starting transfers between devices  17.4 us (8%)
  waiting for transfers between devices  13.2 us (6%)
  other arithmetic  10.5 us (5%)
  local copies, waits for them, and re-layouts  6.63 us (3%)
  between operations  4.8 us (2%)
    all_to_all x2, blocking collectives, prefix(): lax.all_to_all(scan_term[None], 'step', split_axis=1, concat_axis=0, tile...  63.9 us
    all_to_all x2, blocking collectives, prefix(): lax.all_to_all(before_sum, 'step', split_axis=0, concat_axis=1, tiled=True)  51.9 us
    dot_general x8, matrix products, convolve(): jnp.einsum('oj,jfp->ofp', weight[frame_shift], framed[:, frame_shift:fram...  18.6 us
    ppermute x4, waiting for transfers between devices, padded_2(): lax.ppermute(head, axis, [((i + 1) % count, i) for i in range(ends)])  12.2 us
    ppermute x4, starting transfers between devices, padded_2(): lax.ppermute(tail, axis, [(i, (i + 1) % count) for i in range(ends)])  11.8 us
    dot_general x4, matrix products, convolve(): jnp.einsum('oj,jfp->ofp', weight[0], framed[:, 0:frame_count], preferred_...  8.62 us
    psum x1, blocking collectives, local(): norm_total = lax.psum(local_sum, 'space')  6.94 us
    unnamed x28, other arithmetic  6.81 us
  transfers between devices with their start and end apart: 8, of which 5 were waited for; matrix products, arithmetic and copies ran while one was open for 1% of the time, Pallas kernels for 0%

commit v1 on v0

v1 whole, which is shorter than its diff:
```python
import math

import jax
import jax.numpy as jnp
from jax import lax
from jax.experimental import pallas as pl
from jax.experimental.pallas import tpu as pltpu
from jax.sharding import PartitionSpec as P

C = 64
HID = 256
COLS = 80
FRAMES = 4
BF = jnp.bfloat16
F32 = jnp.float32
MESH = pl.DeviceIdType.MESH

PX = 640
OWN = 256
EXT = OWN + PX + 256
Q0 = 128
NQ = 896
HALF = C // 2
TILES = HALF // 8 * (PX // 128)
ALL_TILES = FRAMES * TILES
BLOCKS = PX // 128
CHUNK = 256


def plan(timestep):
    scaled = timestep.astype(F32) / 1000.0
    return -(0.1 * scaled + 9.95 * scaled * scaled)


def coefficients(timestep_pair):
    log_from = plan(timestep_pair[0])
    log_to = plan(timestep_pair[1])
    half_gap = 0.5 * (log_to - log_from)
    decay_gain = jnp.expm1(half_gap)
    remain_from = -jnp.expm1(log_from)
    remain_to = -jnp.expm1(log_to)
    ratio_term = -jnp.expm1(log_from - log_to)
    noise_gain = -jnp.exp(half_gap) * jnp.sqrt(remain_from) + remain_to * jnp.exp(
        -half_gap
    ) / jnp.sqrt(remain_from)
    spread_gain = jnp.sqrt(remain_to / remain_from * ratio_term)
    return jnp.stack([decay_gain, noise_gain, spread_gain])


def time_embed(timestep, time_weight):
    half_count = C // 2
    frequency = jnp.exp(-math.log(10000.0) * jnp.arange(half_count, dtype=F32) / half_count)
    angles = timestep.astype(F32) * frequency
    features = jnp.concatenate([jnp.sin(angles), jnp.cos(angles)])
    return jnp.dot(
        features, time_weight, preferred_element_type=F32, precision=lax.Precision.HIGHEST
    )


def make_kernel(chips, columns_of_space, cell_count):
    slots = -(-ALL_TILES // chips)

    def kernel(
        coef, temb, y_ref, n_ref, w1_ref, w2_ref, out_ref, chg_ref,
        ent, ebf, xc, hid, grp, w1s, w2s,
        st, pb, cs, rx, tx, px, eo, dump, ssq,
        halo_send, halo_recv, pair_send, pair_recv, cs_send, rx_recv, tx_send, px_recv,
        eo_send, ent_recv, ssq_send, ssq_recv,
    ):
        step = lax.axis_index("step")
        space = lax.axis_index("space")
        chip = step // 2
        core = step - 2 * chip
        other = 1 - core
        partner = 2 * chip + other
        anchor = step == 0
        mine_rows = pl.ds(pl.multiple_of(core * HALF, HALF), HALF)
        other_rows = pl.ds(pl.multiple_of(other * HALF, HALF), HALF)

        for s in range(2):
            for f in range(FRAMES):
                ebf[s, f, :, 0:OWN] = jnp.zeros((C, OWN), BF)
                ebf[s, f, :, OWN + PX : EXT] = jnp.zeros((C, OWN), BF)

        barrier = pltpu.get_barrier_semaphore()

        @pl.loop(1, chips)
        def _(d):
            target = lax.rem(chip + d, chips)
            pl.semaphore_signal(
                barrier, inc=1, device_id={"step": 2 * target + core}, device_id_type=MESH
            )

        pl.semaphore_signal(barrier, inc=1, device_id={"step": partner}, device_id_type=MESH)
        for d in range(1, columns_of_space):
            pl.semaphore_signal(
                barrier,
                inc=1,
                device_id={"space": lax.rem(space + d, columns_of_space)},
                device_id_type=MESH,
            )

        lane = lax.broadcasted_iota(jnp.int32, (1, EXT), 1)
        column = lax.rem(lane + (4 * COLS - OWN % COLS), COLS)
        not_last = column != COLS - 1
        not_first = column != 0

        def frame_of(ref, f):
            return jnp.concatenate(
                [ref[pl.ds(b * FRAMES + f, C, stride=BLOCKS * FRAMES), :] for b in range(BLOCKS)],
                axis=1,
            )

        def halo_copies(s, f):
            right = pltpu.make_async_remote_copy(
                src_ref=ebf.at[s, f, :, pl.ds(OWN + PX - 256, 256)],
                dst_ref=ebf.at[s, f, :, pl.ds(0, 256)],
                send_sem=halo_send.at[s, f, 0],
                recv_sem=halo_recv.at[s, f, 0],
                device_id={"space": lax.rem(space + 1, columns_of_space)},
                device_id_type=MESH,
            )
            left = pltpu.make_async_remote_copy(
                src_ref=ebf.at[s, f, :, pl.ds(OWN, 256)],
                dst_ref=ebf.at[s, f, :, pl.ds(OWN + PX, 256)],
                send_sem=halo_send.at[s, f, 1],
                recv_sem=halo_recv.at[s, f, 1],
                device_id={"space": lax.rem(space + columns_of_space - 1, columns_of_space)},
                device_id_type=MESH,
            )
            return right, left

        def halo_start(s, f):
            right, left = halo_copies(s, f)

            @pl.when(space < columns_of_space - 1)
            def _():
                right.start()

            @pl.when(space > 0)
            def _():
                left.start()

        def halo_wait(s, f):
            right, left = halo_copies(s, f)

            @pl.when(space > 0)
            def _():
                right.wait_recv()

            @pl.when(space < columns_of_space - 1)
            def _():
                left.wait_recv()

        def halo_done(s, f):
            right, left = halo_copies(s, f)

            @pl.when(space < columns_of_space - 1)
            def _():
                right.wait_send()

            @pl.when(space > 0)
            def _():
                left.wait_send()

        def im2col(s, f):
            halo_wait(s, f)
            whole = ebf[s, f]
            zero = jnp.zeros_like(whole)
            shifted = (jnp.where(not_last, whole, zero), whole, jnp.where(not_first, whole, zero))
            for b in range(3):
                for c in range(3):
                    start = Q0 + COLS * (b - 1) + (c - 1)
                    row = f * 9 * C + (b * 3 + c) * C
                    xc[row : row + C, :] = shifted[c][:, start : start + NQ]

        def conv_one(f):
            low, high = max(f - 1, 0), min(f + 2, FRAMES)
            first = low - f + 1
            weights = w1s[:, 9 * C * first : 9 * C * (first + high - low)]
            for n in range(0, NQ, CHUNK):
                m = min(n + CHUNK, NQ)
                value = jnp.dot(
                    weights, xc[low * 9 * C : high * 9 * C, n:m], preferred_element_type=F32
                )
                value = value + temb[...]
                value = value / (1.0 + jnp.exp(-value))
                if n + Q0 < OWN:
                    place = lax.broadcasted_iota(jnp.int32, (1, m - n), 1) + (n + Q0)
                    value = jnp.where((place >= OWN) | (space > 0), value, 0.0)
                if m + Q0 > OWN + PX:
                    place = lax.broadcasted_iota(jnp.int32, (1, m - n), 1) + (n + Q0)
                    value = jnp.where(
                        (place < OWN + PX) | (space < columns_of_space - 1), value, 0.0
                    )
                hid[f * HID : (f + 1) * HID, n:m] = value.astype(BF)

        def conv_two(f):
            low, high = max(f - 1, 0), min(f + 2, FRAMES)
            first = low - f + 1
            weights = w2s[:, HID * first : HID * (first + high - low)]
            for n in range(0, NQ, CHUNK):
                m = min(n + CHUNK, NQ)
                grp[:, n:m] = jnp.dot(
                    weights, hid[low * HID : high * HID, n:m], preferred_element_type=F32
                )
            masks = (not_last[:, Q0 : Q0 + NQ], None, not_first[:, Q0 : Q0 + NQ])
            total = None
            for b in range(3):
                for c in range(3):
                    tap = b * 3 + c
                    value = grp[tap * C : (tap + 1) * C, :]
                    if masks[c] is not None:
                        value = jnp.where(masks[c], value, 0.0)
                    start = OWN - Q0 + COLS * (b - 1) + (c - 1)
                    value = pltpu.roll(value, (NQ - start) % NQ, 1)[:, :PX]
                    total = value if total is None else total + value
            return total

        def pair_copy(s, f):
            return pltpu.make_async_remote_copy(
                src_ref=st.at[s, f, other_rows, :],
                dst_ref=pb.at[s, f],
                send_sem=pair_send.at[s, f],
                recv_sem=pair_recv.at[s, f],
                device_id={"step": partner},
                device_id_type=MESH,
            )

        def drift(s, f):
            latent = ent[s, f]
            value = coef[0] * latent + coef[1] * conv_two(f) + coef[2] * frame_of(n_ref, f)
            st[s, f] = value + jnp.where(anchor, latent, 0.0)
            pair_copy(s, f).start()

        def chip_sum(s, f):
            pair_copy(s, f).wait_recv()
            total = st[s, f, mine_rows, :] + pb[s, f]
            for r in range(HALF // 8):
                for b in range(BLOCKS):
                    cs[s, f * TILES + r * BLOCKS + b] = total[
                        8 * r : 8 * r + 8, 128 * b : 128 * b + 128
                    ]

            @pl.loop(f * TILES, (f + 1) * TILES)
            def _(g):
                slot = g // chips
                owner = g - slot * chips

                @pl.when(owner != chip)
                def _():
                    pltpu.make_async_remote_copy(
                        src_ref=cs.at[s, g],
                        dst_ref=rx.at[s, slot, chip],
                        send_sem=cs_send.at[s],
                        recv_sem=rx_recv.at[s, slot],
                        device_id={"step": 2 * owner + core},
                        device_id_type=MESH,
                    ).start()

                @pl.when(owner == chip)
                def _():
                    pltpu.make_async_copy(
                        cs.at[s, g], rx.at[s, slot, chip], rx_recv.at[s, slot]
                    ).start()
                    pltpu.make_async_copy(cs.at[s, g], dump.at[s, slot, 0], cs_send.at[s]).start()

        def own(s, slot):
            tile = slot * chips + chip

            def work():
                pltpu.make_async_copy(rx.at[s, slot], rx.at[s, slot], rx_recv.at[s, slot]).wait()
                running = jnp.zeros((8, 128), F32)
                for q in range(chips):
                    tx[s, slot, q] = running
                    running = running + rx[s, slot, q]
                frame = tile // TILES

                @pl.loop(1, chips)
                def _(d):
                    target = lax.rem(chip + d, chips)
                    pltpu.make_async_remote_copy(
                        src_ref=tx.at[s, slot, target],
                        dst_ref=px.at[s, tile],
                        send_sem=tx_send.at[s, slot],
                        recv_sem=px_recv.at[s, frame],
                        device_id={"step": 2 * target + core},
                        device_id_type=MESH,
                    ).start()

                pltpu.make_async_copy(
                    tx.at[s, slot, chip], px.at[s, tile], px_recv.at[s, frame]
                ).start()
                pltpu.make_async_copy(
                    tx.at[s, slot, chip], dump.at[s, slot, 1], tx_send.at[s, slot]
                ).start()

            if (slot + 1) * chips <= ALL_TILES:
                work()
            else:
                pl.when(tile < ALL_TILES)(work)

        def own_done(s, slot):
            def work():
                pltpu.make_async_copy(tx.at[s, slot], tx.at[s, slot], tx_send.at[s, slot]).wait()

            if (slot + 1) * chips <= ALL_TILES:
                work()
            else:
                pl.when(slot * chips + chip < ALL_TILES)(work)

        def enter_copy(s, f):
            return pltpu.make_async_remote_copy(
                src_ref=eo.at[s, f],
                dst_ref=ent.at[s + 1, f, mine_rows, :],
                send_sem=eo_send.at[s, f],
                recv_sem=ent_recv.at[s, f],
                device_id={"step": partner},
                device_id_type=MESH,
            )

        def enter(s, f):
            tiles = px.at[s, pl.ds(f * TILES, TILES)]
            pltpu.make_async_copy(tiles, tiles, px_recv.at[s, f]).wait()
            before = jnp.concatenate(
                [
                    jnp.concatenate(
                        [px[s, f * TILES + r * BLOCKS + b] for b in range(BLOCKS)], axis=1
                    )
                    for r in range(HALF // 8)
                ],
                axis=0,
            )
            first = jnp.where(core == 0, st[s, f, mine_rows, :], pb[s, f])
            after = before + first
            eo[s, f] = jnp.where(core == 0, after, before)
            enter_copy(s, f).start()
            ent[s + 1, f, mine_rows, :] = jnp.where(core == 0, before, after)

        def entered(s, f):
            copy = enter_copy(s, f)
            pltpu.make_async_copy(
                ent.at[s + 1, f, other_rows, :], ent.at[s + 1, f, other_rows, :], ent_recv.at[s, f]
            ).wait()

            @pl.when(anchor)
            def _():
                ent[s + 1, f] = ent[0, f]

        def latent_out(s, f):
            ebf[s, f, :, OWN : OWN + PX] = ent[s, f].astype(BF)
            halo_start(s, f)

        for f in range(FRAMES):
            ent[0, f] = frame_of(y_ref, f)
        for a in range(3):
            for tap in range(9):
                w2s[tap * C : (tap + 1) * C, a * HID : (a + 1) * HID] = w2_ref[
                    a, :, tap * HID : (tap + 1) * HID
                ]
        w1s[...] = jnp.concatenate([w1_ref[0], w1_ref[1], w1_ref[2]], axis=1)

        pl.semaphore_wait(barrier, chips + columns_of_space - 1)
        for f in range(FRAMES):
            latent_out(0, f)

        for s in range(2):
            im2col(s, 0)
            im2col(s, 1)
            conv_one(0)
            im2col(s, 2)
            conv_one(1)
            drift(s, 0)
            im2col(s, 3)
            conv_one(2)
            chip_sum(s, 0)
            drift(s, 1)
            conv_one(3)
            chip_sum(s, 1)
            drift(s, 2)
            chip_sum(s, 2)
            drift(s, 3)
            chip_sum(s, 3)
            for slot in range(slots):
                own(s, slot)
            for f in range(FRAMES):
                enter(s, f)
            square = None
            for f in range(FRAMES):
                entered(s, f)
                if s == 0:
                    latent_out(1, f)
                else:
                    keep = jnp.where(anchor, 0.0, 1.0)
                    reached = keep * ent[2, f] + st[1, f]
                    change = reached - (keep * ent[1, f] + st[0, f])
                    change = change * change
                    for r in range(C // 8):
                        for b in range(BLOCKS):
                            part = change[8 * r : 8 * r + 8, 128 * b : 128 * b + 128]
                            square = part if square is None else square + part
                    for b in range(BLOCKS):
                        out_ref[pl.ds(b * FRAMES + f, C, stride=BLOCKS * FRAMES), :] = reached[
                            :, 128 * b : 128 * b + 128
                        ]
            if s == 1:
                ssq[0] = square

        def ssq_copy(d):
            return pltpu.make_async_remote_copy(
                src_ref=ssq.at[0],
                dst_ref=ssq.at[columns_of_space + 1 - d],
                send_sem=ssq_send.at[d - 1],
                recv_sem=ssq_recv.at[columns_of_space - 1 - d],
                device_id={"space": lax.rem(space + d, columns_of_space)},
                device_id_type=MESH,
            )

        for d in range(1, columns_of_space):
            ssq_copy(d).start()

        for s in range(2):
            for f in range(FRAMES):
                halo_done(s, f)
                pair_copy(s, f).wait_send()
                enter_copy(s, f).wait_send()
            pltpu.make_async_copy(cs.at[s], cs.at[s], cs_send.at[s]).wait()
            for slot in range(slots):
                own_done(s, slot)

        for d in range(1, columns_of_space):
            ssq_copy(d).wait_send()
        for d in range(1, columns_of_space):
            ssq_copy(columns_of_space - d).wait_recv()
        total = None
        for x in range(columns_of_space):
            part = None
            for d in range(columns_of_space):
                place = 0 if d == 0 else d + 1
                term = jnp.where(lax.rem(space + d, columns_of_space) == x, ssq[place], 0.0)
                part = term if part is None else part + term
            total = part if total is None else total + part
        mean = jnp.sum(total) / cell_count
        chg_ref[...] = jnp.sqrt(jnp.full((8, 128), mean, F32))

    scratch = [
        pltpu.VMEM((3, FRAMES, C, PX), F32),
        pltpu.VMEM((2, FRAMES, C, EXT), BF),
        pltpu.VMEM((FRAMES * 9 * C, NQ), BF),
        pltpu.VMEM((FRAMES * HID, NQ), BF),
        pltpu.VMEM((9 * C, NQ), F32),
        pltpu.VMEM((HID, 27 * C), BF),
        pltpu.VMEM((9 * C, 3 * HID), BF),
        pltpu.VMEM((2, FRAMES, C, PX), F32),
        pltpu.VMEM((2, FRAMES, HALF, PX), F32),
        pltpu.VMEM((2, ALL_TILES, 8, 128), F32),
        pltpu.VMEM((2, slots, chips, 8, 128), F32),
        pltpu.VMEM((2, slots, chips, 8, 128), F32),
        pltpu.VMEM((2, ALL_TILES, 8, 128), F32),
        pltpu.VMEM((2, FRAMES, HALF, PX), F32),
        pltpu.VMEM((2, slots, 2, 8, 128), F32),
        pltpu.VMEM((columns_of_space + 1, 8, 128), F32),
        pltpu.SemaphoreType.DMA((2, FRAMES, 2)),
        pltpu.SemaphoreType.DMA((2, FRAMES, 2)),
        pltpu.SemaphoreType.DMA((2, FRAMES)),
        pltpu.SemaphoreType.DMA((2, FRAMES)),
        pltpu.SemaphoreType.DMA((2,)),
        pltpu.SemaphoreType.DMA((2, slots)),
        pltpu.SemaphoreType.DMA((2, slots)),
        pltpu.SemaphoreType.DMA((2, FRAMES)),
        pltpu.SemaphoreType.DMA((2, FRAMES)),
        pltpu.SemaphoreType.DMA((2, FRAMES)),
        pltpu.SemaphoreType.DMA((columns_of_space,)),
        pltpu.SemaphoreType.DMA((columns_of_space,)),
    ]
    return kernel, scratch


def solution(mesh):
    steps, spaces = mesh.shape["step"], mesh.shape["space"]
    cell_count = float(C * FRAMES * PX * spaces)
    kernel, scratch = make_kernel(steps // 2, spaces, cell_count)

    def flat(array):
        cells = array.reshape(C, FRAMES, BLOCKS, 128).transpose(0, 2, 1, 3)
        return cells.reshape(C * BLOCKS * FRAMES, 128)

    def local(guesses, noise, timesteps, conv_first, conv_second, time_weight):
        coef = coefficients(timesteps[0])
        temb = time_embed(timesteps[0, 0], time_weight)[:, None]
        vmem = pl.BlockSpec(memory_space=pltpu.VMEM)
        states, changes = pl.pallas_call(
            kernel,
            out_shape=(
                jax.ShapeDtypeStruct((C * BLOCKS * FRAMES, 128), F32),
                jax.ShapeDtypeStruct((8, 128), F32),
            ),
            in_specs=[pl.BlockSpec(memory_space=pltpu.SMEM)] + [vmem] * 5,
            out_specs=(vmem, vmem),
            scratch_shapes=scratch,
            compiler_params=pltpu.CompilerParams(
                collective_id=0, has_side_effects=True, vmem_limit_bytes=56 * 2**20
            ),
        )(coef, temb, flat(guesses[0]), flat(noise[0]), conv_first, conv_second)
        states = states.reshape(C, BLOCKS, FRAMES, 128).transpose(0, 2, 1, 3)
        return states.reshape(1, C, FRAMES, PX), changes[0, :1]

    in_specs = (
        P("step", None, None, "space"),
        P("step", None, None, "space"),
        P("step", None),
        P(),
        P(),
        P(),
    )
    out_specs = (P("step", None, None, "space"), P("step"))
    return jax.shard_map(local, mesh=mesh, in_specs=in_specs, out_specs=out_specs, check_vma=False)
```

time: 205 us -> 94.8 us (0.46)
  blocking collectives: 123 us -> 0 us
  Pallas kernels: 0 us -> 79.9 us
  matrix products: 28.4 us -> 1.06 us
  starting transfers between devices: 17.4 us -> 0 us
  waiting for transfers between devices: 13.2 us -> 0 us
  other arithmetic: 10.5 us -> 0.66 us
  local copies, waits for them, and re-layouts: 6.63 us -> 10.5 us
  between operations: 4.8 us -> 2.45 us
    all_to_all x4 -> x0, blocking collectives: 116 us -> none  [the longest x2 63.9 us: prefix(): lax.all_to_all(scan_term[None], 'step', split_axis=1, concat_axis=0, tile...]
    pallas_call x0 -> x1, Pallas kernels: none -> 79.9 us  [local(): pl.pallas_call(kernel, out_shape=(jax.ShapeDtypeStruct((C * BLOCKS * FRAM...]
    dot_general x15 -> x1, matrix products: 28.4 us -> 1.06 us  [time_embed(): jnp.dot(features, time_weight, preferred_element_type=F32, precision=lax....]
    ppermute x8 -> x0, starting transfers between devices: 17.4 us -> none  [the longest x4 11.8 us: padded_2(): lax.ppermute(tail, axis, [(i, (i + 1) % count) for i in range(ends)])]
    ppermute x8 -> x0, waiting for transfers between devices: 13.2 us -> none  [the longest x4 12.2 us: padded_2(): lax.ppermute(head, axis, [((i + 1) % count, i) for i in range(ends)])]
    psum x1 -> x0, blocking collectives: 6.94 us -> none  [local(): norm_total = lax.psum(local_sum, 'space')]
    unnamed x28 -> x0, other arithmetic: 6.81 us -> none
    concatenate x8 -> x0, other arithmetic: 2.61 us -> none  [the longest x4 1.4 us: padded_2(): jnp.concatenate([lax.ppermute(tail, axis, [(i, (i + 1) % count) for i in...]
  transfers between devices with their start and end apart: 8 -> 0, of which waited for: 5 -> 0; matrix products, arithmetic and copies ran while one was open for 1% -> 0% of each run, Pallas kernels for 0% -> 0%
where the time goes in v1:
time: 94.8 us; the launch traced here: 94.5 us
  Pallas kernels  79.9 us (84%)
  local copies, waits for them, and re-layouts  10.5 us (11%)
  between operations  2.45 us (3%)
  matrix products  1.06 us (1%)
    pallas_call x1, Pallas kernels, local(): pl.pallas_call(kernel, out_shape=(jax.ShapeDtypeStruct((C * BLOCKS * FRAM...  79.9 us
    unnamed x10, local copies, waits for them, and re-layouts  3.81 us
    transpose x2, local copies, waits for them, and re-layouts, flat(): cells = array.reshape(C, FRAMES, BLOCKS, 128).transpose(0, 2, 1, 3)  2.55 us

profile of v1, /device:TPU:1, one launch (start us, length us, event | category | flops | bytes accessed | tf_op | source)
XLA Modules:
  0.0 94.5 jit_solution(2630930671687524728)
XLA Ops:
  0.6 0.0 copy-start
  0.6 1.3 %fusion.5 = (s32[1,1]{1,0:T(1,128)}, s32[1,1]{1,0:T(1,128)}) fusion(s32[1,2]{1,0:T(1,128)} %param.8), kind=kLoop, calls=%fused_computation.10 | loop fusion | bytes 16 | tf_op jit(solution)/shard_map/slice | solution.py:36
  3.7 0.6 pad_maximum_fusion.coef
  4.4 0.0 copy-done
  4.4 1.1 %convolution_bitcast_fusion.temb = f32[256,1]{1,0:T(8,128)} fusion(f32[64,256]{1,0:T(8,128)S(1)} %copy-done, f32[32]{0:T(128)S(1)} %get-tuple-element.10, f32[32]{0:T(128)S(1)} %get-tuple-element.11), kind=kOutput, calls=%fused_computation | convolution fusion | flops 196672 | bytes 66816 | tf_op jit(solution)/shard_map/dot_general | solution.py:55
  5.4 1.1 %copy.12 = f32[1,64,4,640]{3,1,2,0:T(8,128)S(1)} copy(f32[1,64,4,640]{3,2,1,0:T(4,128)} %param.6) | data formatting | bytes 1310720 | tf_op args[0]
  6.6 0.1 reshape_squeeze.6
  6.7 0.0 copy-start.2
  6.7 1.3 %copy.13 = f32[64,5,4,128]{3,2,1,0:T(4,128)} copy(f32[64,5,4,128]{3,1,0,2:T(8,128)S(1)} %bitcast.32) | data formatting | bytes 1310720 | tf_op jit(solution)/shard_map/transpose | solution.py:485
  7.9 0.0 copy-done.2
  8.0 0.1 reshape_squeeze.7
  8.1 0.0 copy-start.1
  8.1 1.3 %copy.15 = f32[64,5,4,128]{3,2,1,0:T(4,128)} copy(f32[64,5,4,128]{3,1,0,2:T(8,128)S(1)} %bitcast.33) | data formatting | bytes 1310720 | tf_op jit(solution)/shard_map/transpose | solution.py:485
  9.4 0.0 copy-done.1
  9.4 1.4 %copy.17.w1_ref = bf16[3,256,576]{2,1,0:T(8,128)(2,1)} copy(bf16[3,256,576]{1,2,0:T(8,128)(2,1)S(1)} %copy-done.1) | data formatting | bytes 1769472 | tf_op args[3]
  10.8 79.9 %shard_map.77 = (f32[1280,128]{1,0:T(8,128)}, f32[8,128]{1,0:T(8,128)}) custom-call(f32[3]{0:T(128)} %pad_maximum_fusion.coef, f32[256,1]{1,0:T(8,128)} %convolution_bitcast_fusion.temb, f32[1280,128]{1,0:T(8,128)} %bitcast.35, f32[1280,128]{1,0:T(8,128)} %bitcast.36, bf16[3,256,576]{2,1,0:T(8,128)(2,1)} %copy.17.w1_ref, bf16[3,64,2304]{2,1,0:T(8,128)(2,1)} %w2_ref.1), custom_call_target="tpu_custom_call" | custom-call | tf_op jit(solution)/shard_map/pallas_call | solution.py:492
  90.6 1.2 %slice.14 = f32[1,1]{1,0:T(1,128)} slice(f32[8,128]{1,0:T(8,128)} %get-tuple-element.5), slice={[0:1], [0:1]} | slice | bytes 8 | tf_op jit(solution)/shard_map/slice | solution.py:506
  91.8 1.2 %copy.21 = f32[64,5,4,128]{3,1,0,2:T(8,128)S(1)} copy(f32[64,5,4,128]{3,2,1,0:T(4,128)} %bitcast.37) | data formatting | bytes 1310720 | tf_op jit(solution)/shard_map/reshape | solution.py:505
  93.0 0.2 reshape.31
  93.2 1.3 %copy.19 = f32[1,64,4,640]{3,2,1,0:T(4,128)} copy(f32[1,64,4,640]{3,1,2,0:T(8,128)S(1)} %reshape.31) | data formatting | bytes 1310720
  (2 shorter events, 0.1 us)
Async XLA Ops:
  0.6 3.7 %copy-start = (f32[64,256]{1,0:T(8,128)S(1)}, f32[64,256]{1,0:T(8,128)}, u32[]{:S(2)}) copy-start(f32[64,256]{1,0:T(8,128)} %param.11) | copy-start | bytes 196612
  6.7 1.3 %copy-start.2 = (f32[1,64,4,640]{3,2,1,0:T(4,128)S(1)}, f32[1,64,4,640]{3,2,1,0:T(4,128)}, u32[]{:S(2)}) copy-start(f32[1,64,4,640]{3,2,1,0:T(4,128)} %param.7) | copy-start | bytes 1966084
  8.1 1.3 %copy-start.1 = (bf16[3,256,576]{1,2,0:T(8,128)(2,1)S(1)}, bf16[3,256,576]{1,2,0:T(8,128)(2,1)}, u32[]{:S(2)}) copy-start(bf16[3,256,576]{1,2,0:T(8,128)(2,1)} %param.9) | copy-start | bytes 2654212

commit v2 on v1

--- a/solution.py
+++ b/solution.py
@@ -22,48 +22,44 @@
 NQ = 896
 HALF = C // 2
 TILES = HALF // 8 * (PX // 128)
-ALL_TILES = FRAMES * TILES
 BLOCKS = PX // 128
 CHUNK = 256
 
 
+def expm1(value):
+    series = 1.0 + value / 11.0
+    for n in range(10, 1, -1):
+        series = 1.0 + value / n * series
+    return jnp.where(jnp.abs(value) < 0.5, value * series, jnp.exp(value) - 1.0)
+
+
 def plan(timestep):
-    scaled = timestep.astype(F32) / 1000.0
+    scaled = timestep / 1000.0
     return -(0.1 * scaled + 9.95 * scaled * scaled)
 
 
-def coefficients(timestep_pair):
-    log_from = plan(timestep_pair[0])
-    log_to = plan(timestep_pair[1])
+def coefficients(before, after):
+    log_from = plan(before)
+    log_to = plan(after)
     half_gap = 0.5 * (log_to - log_from)
-    decay_gain = jnp.expm1(half_gap)
-    remain_from = -jnp.expm1(log_from)
-    remain_to = -jnp.expm1(log_to)
-    ratio_term = -jnp.expm1(log_from - log_to)
+    decay_gain = expm1(half_gap)
+    remain_from = -expm1(log_from)
+    remain_to = -expm1(log_to)
+    ratio_term = -expm1(log_from - log_to)
     noise_gain = -jnp.exp(half_gap) * jnp.sqrt(remain_from) + remain_to * jnp.exp(
         -half_gap
     ) / jnp.sqrt(remain_from)
     spread_gain = jnp.sqrt(remain_to / remain_from * ratio_term)
-    return jnp.stack([decay_gain, noise_gain, spread_gain])
-
-
-def time_embed(timestep, time_weight):
-    half_count = C // 2
-    frequency = jnp.exp(-math.log(10000.0) * jnp.arange(half_count, dtype=F32) / half_count)
-    angles = timestep.astype(F32) * frequency
-    features = jnp.concatenate([jnp.sin(angles), jnp.cos(angles)])
-    return jnp.dot(
-        features, time_weight, preferred_element_type=F32, precision=lax.Precision.HIGHEST
-    )
+    return decay_gain, noise_gain, spread_gain
 
 
 def make_kernel(chips, columns_of_space, cell_count):
-    slots = -(-ALL_TILES // chips)
+    parts = -(-TILES // chips)
 
     def kernel(
-        coef, temb, y_ref, n_ref, w1_ref, w2_ref, out_ref, chg_ref,
-        ent, ebf, xc, hid, grp, w1s, w2s,
-        st, pb, cs, rx, tx, px, eo, dump, ssq,
+        times, y_hbm, n_hbm, w1_hbm, w2_hbm, tw_hbm, out_hbm, chg_ref,
+        ent, ebf, xc, hid, grp, w1r, w2r, twr, w1s, w2s, temb, noise, res,
+        st, pb, cs, rx, tx, px, eo, ssq, load_sem, out_sem,
         halo_send, halo_recv, pair_send, pair_recv, cs_send, rx_recv, tx_send, px_recv,
         eo_send, ent_recv, ssq_send, ssq_recv,
     ):
@@ -77,6 +73,19 @@
         mine_rows = pl.ds(pl.multiple_of(core * HALF, HALF), HALF)
         other_rows = pl.ds(pl.multiple_of(other * HALF, HALF), HALF)
 
+        loads = [pltpu.make_async_copy(y_hbm.at[:, f, :], ent.at[0, f], load_sem.at[f]) for f in range(FRAMES)]
+        loads += [
+            pltpu.make_async_copy(n_hbm.at[:, f, :], noise.at[f], load_sem.at[FRAMES + f])
+            for f in range(FRAMES)
+        ]
+        late = [
+            pltpu.make_async_copy(tw_hbm, twr, load_sem.at[2 * FRAMES]),
+            pltpu.make_async_copy(w1_hbm, w1r, load_sem.at[2 * FRAMES + 1]),
+            pltpu.make_async_copy(w2_hbm, w2r, load_sem.at[2 * FRAMES + 2]),
+        ]
+        for copy in loads[:FRAMES] + late + loads[FRAMES:]:
+            copy.start()
+
         for s in range(2):
             for f in range(FRAMES):
                 ebf[s, f, :, 0:OWN] = jnp.zeros((C, OWN), BF)
@@ -104,12 +113,6 @@
         column = lax.rem(lane + (4 * COLS - OWN % COLS), COLS)
         not_last = column != COLS - 1
         not_first = column != 0
-
-        def frame_of(ref, f):
-            return jnp.concatenate(
-                [ref[pl.ds(b * FRAMES + f, C, stride=BLOCKS * FRAMES), :] for b in range(BLOCKS)],
-                axis=1,
-            )
 
         def halo_copies(s, f):
             right = pltpu.make_async_remote_copy(
@@ -183,7 +186,7 @@
                 value = jnp.dot(
                     weights, xc[low * 9 * C : high * 9 * C, n:m], preferred_element_type=F32
                 )
-                value = value + temb[...]
+                value = value + jnp.concatenate([temb[...]] * ((m - n) // 128), axis=1)
                 value = value / (1.0 + jnp.exp(-value))
                 if n + Q0 < OWN:
                     place = lax.broadcasted_iota(jnp.int32, (1, m - n), 1) + (n + Q0)
@@ -229,7 +232,7 @@
 
         def drift(s, f):
             latent = ent[s, f]
-            value = coef[0] * latent + coef[1] * conv_two(f) + coef[2] * frame_of(n_ref, f)
+            value = decay_gain * latent + noise_gain * conv_two(f) + spread_gain * noise[f]
             st[s, f] = value + jnp.where(anchor, latent, 0.0)
             pair_copy(s, f).start()
 
@@ -238,76 +241,93 @@
             total = st[s, f, mine_rows, :] + pb[s, f]
             for r in range(HALF // 8):
                 for b in range(BLOCKS):
-                    cs[s, f * TILES + r * BLOCKS + b] = total[
-                        8 * r : 8 * r + 8, 128 * b : 128 * b + 128
-                    ]
-
-            @pl.loop(f * TILES, (f + 1) * TILES)
-            def _(g):
-                slot = g // chips
-                owner = g - slot * chips
-
-                @pl.when(owner != chip)
-                def _():
-                    pltpu.make_async_remote_copy(
-                        src_ref=cs.at[s, g],
-                        dst_ref=rx.at[s, slot, chip],
-                        send_sem=cs_send.at[s],
-                        recv_sem=rx_recv.at[s, slot],
-                        device_id={"step": 2 * owner + core},
-                        device_id_type=MESH,
-                    ).start()
-
-                @pl.when(owner == chip)
-                def _():
-                    pltpu.make_async_copy(
-                        cs.at[s, g], rx.at[s, slot, chip], rx_recv.at[s, slot]
-                    ).start()
-                    pltpu.make_async_copy(cs.at[s, g], dump.at[s, slot, 0], cs_send.at[s]).start()
-
-        def own(s, slot):
-            tile = slot * chips + chip
-
-            def work():
-                pltpu.make_async_copy(rx.at[s, slot], rx.at[s, slot], rx_recv.at[s, slot]).wait()
-                running = jnp.zeros((8, 128), F32)
-                for q in range(chips):
-                    tx[s, slot, q] = running
-                    running = running + rx[s, slot, q]
-                frame = tile // TILES
-
-                @pl.loop(1, chips)
-                def _(d):
-                    target = lax.rem(chip + d, chips)
-                    pltpu.make_async_remote_copy(
-                        src_ref=tx.at[s, slot, target],
-                        dst_ref=px.at[s, tile],
-                        send_sem=tx_send.at[s, slot],
-                        recv_sem=px_recv.at[s, frame],
-                        device_id={"step": 2 * target + core},
-                        device_id_type=MESH,
-                    ).start()
-
-                pltpu.make_async_copy(
-                    tx.at[s, slot, chip], px.at[s, tile], px_recv.at[s, frame]
-                ).start()
-                pltpu.make_async_copy(
-                    tx.at[s, slot, chip], dump.at[s, slot, 1], tx_send.at[s, slot]
-                ).start()
-
-            if (slot + 1) * chips <= ALL_TILES:
-                work()
+                    cs[s, f, r * BLOCKS + b] = total[8 * r : 8 * r + 8, 128 * b : 128 * b + 128]
+            for k in range(parts):
+                low, high, base = span(f, k)
+
+                @pl.loop(low, high)
+                def _(g):
+                    owner = g + base
+                    owner = jnp.where(owner >= chips, owner - chips, owner)
+
+                    @pl.when(owner != chip)
+                    def _():
+                        pltpu.make_async_remote_copy(
+                            src_ref=cs.at[s, f, g],
+                            dst_ref=rx.at[s, f, k, chip],
+                            send_sem=cs_send.at[s, f, k],
+                            recv_sem=rx_recv.at[s, f, k],
+                            device_id={"step": 2 * owner + core},
+                            device_id_type=MESH,
+                        ).start()
+
+                def keep(g):
+                    rx[s, f, k, chip] = cs[s, f, g]
+
+                if_mine(f, k, keep)
+
+        def own(s, f):
+            for k in range(parts):
+
+                def work(g):
+                    given = rx.at[s, f, k, pl.ds(0, chips - 1)]
+                    pltpu.make_async_copy(given, given, rx_recv.at[s, f, k]).wait()
+                    running = jnp.zeros((8, 128), F32)
+                    for q in range(chips):
+                        tx[s, f, k, q] = running
+                        running = running + rx[s, f, k, q]
+
+                    @pl.loop(1, chips)
+                    def _(d):
+                        target = chip + d
+                        target = jnp.where(target >= chips, target - chips, target)
+                        pltpu.make_async_remote_copy(
+                            src_ref=tx.at[s, f, k, target],
+                            dst_ref=px.at[s, f, g],
+                            send_sem=tx_send.at[s, f, k],
+                            recv_sem=px_recv.at[s, f, k],
+                            device_id={"step": 2 * target + core},
+                            device_id_type=MESH,
+                        ).start()
+
+                    px[s, f, g] = tx[s, f, k, chip]
+
+                if_mine(f, k, work)
+
+        def span(f, k):
+            low, high = k * chips, min((k + 1) * chips, TILES)
+            return low, high, f * TILES % chips - low
+
+        def if_mine(f, k, work, otherwise=None):
+            low, high, base = span(f, k)
+            g = chip - base
+            g = jnp.where(g < low, g + chips, g)
+            if high - low == chips:
+                work(g)
             else:
-                pl.when(tile < ALL_TILES)(work)
-
-        def own_done(s, slot):
-            def work():
-                pltpu.make_async_copy(tx.at[s, slot], tx.at[s, slot], tx_send.at[s, slot]).wait()
-
-            if (slot + 1) * chips <= ALL_TILES:
-                work()
-            else:
-                pl.when(slot * chips + chip < ALL_TILES)(work)
+                pl.when(g < high)(lambda: work(g))
+                if otherwise is not None:
+                    pl.when(g >= high)(lambda: otherwise(g))
+
+        def tiles_wait(ref, sem, s, f):
+            for k in range(parts):
+                low, high, _ = span(f, k)
+
+                def wait(count):
+                    tiles = ref.at[s, f, pl.ds(0, count)]
+                    return lambda g: pltpu.make_async_copy(tiles, tiles, sem.at[s, f, k]).wait()
+
+                if_mine(f, k, wait(high - low - 1), wait(high - low))
+
+        def scan_done(s, f):
+            tiles_wait(cs, cs_send, s, f)
+            for k in range(parts):
+
+                def wait(g):
+                    sent = tx.at[s, f, k, pl.ds(0, chips - 1)]
+                    pltpu.make_async_copy(sent, sent, tx_send.at[s, f, k]).wait()
+
+                if_mine(f, k, wait)
 
         def enter_copy(s, f):
             return pltpu.make_async_remote_copy(
@@ -320,12 +340,11 @@
             )
 
         def enter(s, f):
-            tiles = px.at[s, pl.ds(f * TILES, TILES)]
-            pltpu.make_async_copy(tiles, tiles, px_recv.at[s, f]).wait()
+            tiles_wait(px, px_recv, s, f)
             before = jnp.concatenate(
                 [
                     jnp.concatenate(
-                        [px[s, f * TILES + r * BLOCKS + b] for b in range(BLOCKS)], axis=1
+                        [px[s, f, r * BLOCKS + b] for b in range(BLOCKS)], axis=1
                     )
                     for r in range(HALF // 8)
                 ],
@@ -338,7 +357,6 @@
             ent[s + 1, f, mine_rows, :] = jnp.where(core == 0, before, after)
 
         def entered(s, f):
-            copy = enter_copy(s, f)
             pltpu.make_async_copy(
                 ent.at[s + 1, f, other_rows, :], ent.at[s + 1, f, other_rows, :], ent_recv.at[s, f]
             ).wait()
@@ -351,18 +369,44 @@
             ebf[s, f, :, OWN : OWN + PX] = ent[s, f].astype(BF)
             halo_start(s, f)
 
+        before = jnp.full((8, 128), times[0, 0], jnp.int32).astype(F32)
+        after = jnp.full((8, 128), times[0, 1], jnp.int32).astype(F32)
+        decay_gain, noise_gain, spread_gain = [
+            gain[0:1, 0:1] for gain in coefficients(before, after)
+        ]
+        index = lax.broadcasted_iota(jnp.int32, (C, 128), 0)
+        sine = index < C // 2
+        place = jnp.where(sine, index, index - C // 2).astype(F32)
+        frequency = jnp.exp(-math.log(10000.0) * place / (C // 2))
+        angles = before[0:1, :] * frequency
+        features = jnp.where(sine, jnp.sin(angles), jnp.cos(angles))
+        for copy in loads[:FRAMES]:
+            copy.wait()
         for f in range(FRAMES):
-            ent[0, f] = frame_of(y_ref, f)
+            ebf[0, f, :, OWN : OWN + PX] = ent[0, f].astype(BF)
+        late[0].wait()
+        for n in range(0, HID, 128):
+            row = jnp.sum(twr[:, n : n + 128] * features, axis=0, keepdims=True)
+            temb[n : n + 128, :] = jnp.broadcast_to(row, (128, 128)).T
+        late[1].wait()
+        for n in range(0, 27 * C, 128):
+            m = min(n + 128, 27 * C)
+            w1s[:, n:m] = w1r[n:m, :].T
+        late[2].wait()
         for a in range(3):
             for tap in range(9):
-                w2s[tap * C : (tap + 1) * C, a * HID : (a + 1) * HID] = w2_ref[
+                w2s[tap * C : (tap + 1) * C, a * HID : (a + 1) * HID] = w2r[
                     a, :, tap * HID : (tap + 1) * HID
                 ]
-        w1s[...] = jnp.concatenate([w1_ref[0], w1_ref[1], w1_ref[2]], axis=1)
+        for copy in loads[FRAMES:]:
+            copy.wait()
 
         pl.semaphore_wait(barrier, chips + columns_of_space - 1)
         for f in range(FRAMES):
-            latent_out(0, f)
+            halo_start(0, f)
+
+        def out_copy(f):
+            return pltpu.make_async_copy(res.at[f], out_hbm.at[:, f, :], out_sem.at[f])
 
         for s in range(2):
             im2col(s, 0)
@@ -381,12 +425,13 @@
             chip_sum(s, 2)
             drift(s, 3)
             chip_sum(s, 3)
-            for slot in range(slots):
-                own(s, slot)
             for f in range(FRAMES):
-                enter(s, f)
+                own(s, f)
             square = None
+            enter(s, 0)
             for f in range(FRAMES):
+                if f + 1 < FRAMES:
+                    enter(s, f + 1)
                 entered(s, f)
                 if s == 0:
                     latent_out(1, f)
@@ -399,10 +444,8 @@
                         for b in range(BLOCKS):
                             part = change[8 * r : 8 * r + 8, 128 * b : 128 * b + 128]
                             square = part if square is None else square + part
-                    for b in range(BLOCKS):
-                        out_ref[pl.ds(b * FRAMES + f, C, stride=BLOCKS * FRAMES), :] = reached[
-                            :, 128 * b : 128 * b + 128
-                        ]
+                    res[f] = reached
+                    out_copy(f).start()
             if s == 1:
                 ssq[0] = square
 
@@ -424,9 +467,9 @@
                 halo_done(s, f)
                 pair_copy(s, f).wait_send()
                 enter_copy(s, f).wait_send()
-            pltpu.make_async_copy(cs.at[s], cs.at[s], cs_send.at[s]).wait()
-            for slot in range(slots):
-                own_done(s, slot)
+                scan_done(s, f)
+        for f in range(FRAMES):
+            out_copy(f).wait()
 
         for d in range(1, columns_of_space):
             ssq_copy(d).wait_send()
@@ -440,8 +483,8 @@
                 term = jnp.where(lax.rem(space + d, columns_of_space) == x, ssq[place], 0.0)
                 part = term if part is None else part + term
             total = part if total is None else total + part
-        mean = jnp.sum(total) / cell_count
-        chg_ref[...] = jnp.sqrt(jnp.full((8, 128), mean, F32))
+        mean = jnp.full((8, 128), jnp.sum(total), F32) / cell_count
+        chg_ref[0] = jnp.max(jnp.sqrt(mean))
 
     scratch = [
         pltpu.VMEM((3, FRAMES, C, PX), F32),
@@ -449,25 +492,32 @@
         pltpu.VMEM((FRAMES * 9 * C, NQ), BF),
         pltpu.VMEM((FRAMES * HID, NQ), BF),
         pltpu.VMEM((9 * C, NQ), F32),
+        pltpu.VMEM((27 * C, HID), BF),
+        pltpu.VMEM((3, C, 9 * HID), BF),
+        pltpu.VMEM((C, HID), F32),
         pltpu.VMEM((HID, 27 * C), BF),
         pltpu.VMEM((9 * C, 3 * HID), BF),
+        pltpu.VMEM((HID, 128), F32),
+        pltpu.VMEM((FRAMES, C, PX), F32),
+        pltpu.VMEM((FRAMES, C, PX), F32),
         pltpu.VMEM((2, FRAMES, C, PX), F32),
         pltpu.VMEM((2, FRAMES, HALF, PX), F32),
-        pltpu.VMEM((2, ALL_TILES, 8, 128), F32),
-        pltpu.VMEM((2, slots, chips, 8, 128), F32),
-        pltpu.VMEM((2, slots, chips, 8, 128), F32),
-        pltpu.VMEM((2, ALL_TILES, 8, 128), F32),
+        pltpu.VMEM((2, FRAMES, TILES, 8, 128), F32),
+        pltpu.VMEM((2, FRAMES, parts, chips, 8, 128), F32),
+        pltpu.VMEM((2, FRAMES, parts, chips, 8, 128), F32),
+        pltpu.VMEM((2, FRAMES, TILES, 8, 128), F32),
         pltpu.VMEM((2, FRAMES, HALF, PX), F32),
-        pltpu.VMEM((2, slots, 2, 8, 128), F32),
         pltpu.VMEM((columns_of_space + 1, 8, 128), F32),
+        pltpu.SemaphoreType.DMA((2 * FRAMES + 3,)),
+        pltpu.SemaphoreType.DMA((FRAMES,)),
         pltpu.SemaphoreType.DMA((2, FRAMES, 2)),
         pltpu.SemaphoreType.DMA((2, FRAMES, 2)),
         pltpu.SemaphoreType.DMA((2, FRAMES)),
         pltpu.SemaphoreType.DMA((2, FRAMES)),
-        pltpu.SemaphoreType.DMA((2,)),
-        pltpu.SemaphoreType.DMA((2, slots)),
-        pltpu.SemaphoreType.DMA((2, slots)),
-        pltpu.SemaphoreType.DMA((2, FRAMES)),
+        pltpu.SemaphoreType.DMA((2, FRAMES, parts)),
+        pltpu.SemaphoreType.DMA((2, FRAMES, parts)),
+        pltpu.SemaphoreType.DMA((2, FRAMES, parts)),
+        pltpu.SemaphoreType.DMA((2, FRAMES, parts)),
         pltpu.SemaphoreType.DMA((2, FRAMES)),
         pltpu.SemaphoreType.DMA((2, FRAMES)),
         pltpu.SemaphoreType.DMA((columns_of_space,)),
@@ -481,29 +531,24 @@
     cell_count = float(C * FRAMES * PX * spaces)
     kernel, scratch = make_kernel(steps // 2, spaces, cell_count)
 
-    def flat(array):
-        cells = array.reshape(C, FRAMES, BLOCKS, 128).transpose(0, 2, 1, 3)
-        return cells.reshape(C * BLOCKS * FRAMES, 128)
-
     def local(guesses, noise, timesteps, conv_first, conv_second, time_weight):
-        coef = coefficients(timesteps[0])
-        temb = time_embed(timesteps[0, 0], time_weight)[:, None]
-        vmem = pl.BlockSpec(memory_space=pltpu.VMEM)
+        anywhere = pl.BlockSpec(memory_space=pl.ANY)
+        scalars = pl.BlockSpec(memory_space=pltpu.SMEM)
+        first = conv_first.transpose(0, 2, 1).reshape(27 * C, HID)
         states, changes = pl.pallas_call(
             kernel,
             out_shape=(
-                jax.ShapeDtypeStruct((C * BLOCKS * FRAMES, 128), F32),
-                jax.ShapeDtypeStruct((8, 128), F32),
+                jax.ShapeDtypeStruct((C, FRAMES, PX), F32),
+                jax.ShapeDtypeStruct((1,), F32),
             ),
-            in_specs=[pl.BlockSpec(memory_space=pltpu.SMEM)] + [vmem] * 5,
-            out_specs=(vmem, vmem),
+            in_specs=[scalars] + [anywhere] * 5,
+            out_specs=(anywhere, scalars),
             scratch_shapes=scratch,
             compiler_params=pltpu.CompilerParams(
                 collective_id=0, has_side_effects=True, vmem_limit_bytes=56 * 2**20
             ),
-        )(coef, temb, flat(guesses[0]), flat(noise[0]), conv_first, conv_second)
-        states = states.reshape(C, BLOCKS, FRAMES, 128).transpose(0, 2, 1, 3)
-        return states.reshape(1, C, FRAMES, PX), changes[0, :1]
+        )(timesteps, guesses[0], noise[0], first, conv_second, time_weight)
+        return states[None], changes
 
     in_specs = (
         P("step", None, None, "space"),

time: 94.8 us -> 80.5 us (0.85)
  local copies, waits for them, and re-layouts: 10.5 us -> 1.98 us
  Pallas kernels: 79.9 us -> 76 us
  matrix products: 1.06 us -> 0 us
    pallas_call x1, Pallas kernels: 79.9 us -> 76 us  [local(): pl.pallas_call(kernel, out_shape=(jax.ShapeDtypeStruct((C, FRAMES, PX), F...]
    transpose x2 -> x0, local copies, waits for them, and re-layouts: 2.55 us -> none  [flat(): cells = array.reshape(C, FRAMES, BLOCKS, 128).transpose(0, 2, 1, 3)]
    slice x2 -> x0, local copies, waits for them, and re-layouts: 2.49 us -> none  [the longest x1 1.31 us: coefficients(): log_from = plan(timestep_pair[0])]
    unnamed x10 -> x1, local copies, waits for them, and re-layouts: 3.81 us -> 1.98 us
    reshape x2 -> x0, local copies, waits for them, and re-layouts: 1.4 us -> none  [the longest x1 1.22 us: local(): states = states.reshape(C, BLOCKS, FRAMES, 128).transpose(0, 2, 1, 3)]
    dot_general x1 -> x0, matrix products: 1.06 us -> none  [time_embed(): jnp.dot(features, time_weight, preferred_element_type=F32, precision=lax....]
where the time goes in v2:
time: 80.5 us; the launch traced here: 80.4 us
  Pallas kernels  76 us (94%)
  between operations  2.39 us (3%)
  local copies, waits for them, and re-layouts  1.98 us (2%)
    pallas_call x1, Pallas kernels, local(): pl.pallas_call(kernel, out_shape=(jax.ShapeDtypeStruct((C, FRAMES, PX), F...  76 us
    unnamed x1, local copies, waits for them, and re-layouts  1.98 us

profile of v2, /device:TPU:1, one launch (start us, length us, event | category | flops | bytes accessed | tf_op | source)
XLA Modules:
  0.0 80.4 jit_solution(5089307235389831081)
XLA Ops:
  0.6 76.0 %shard_map.77 = (f32[64,4,640]{2,1,0:T(4,128)}, f32[1]{0:T(128)}) custom-call(s32[1,2]{1,0:T(1,128)} %times.1, f32[64,4,640]{2,1,0:T(4,128)} %bitcast.8, f32[64,4,640]{2,1,0:T(4,128)} %bitcast.9, bf16[1728,256]{1,0:T(8,128)(2,1)} %bitcast.6, bf16[3,64,2304]{2,1,0:T(8,128)(2,1)} %w2_hbm.1, f32[64,256]{1,0:T(8,128)} %tw_hbm.1), custom_call_target="tpu_custom_call" | custom-call | tf_op jit(solution)/shard_map/pallas_call | solution.py:538
  76.6 2.0 %copy.10 = f32[1,64,4,640]{3,2,1,0:T(4,128)} copy(f32[1,64,4,640]{3,2,1,0:T(4,128)} %bitcast.7) | data formatting | bytes 1310720

commit v3 on v2

--- a/solution.py
+++ b/solution.py
@@ -55,11 +55,14 @@
 
 def make_kernel(chips, columns_of_space, cell_count):
     parts = -(-TILES // chips)
+    wide = min(4, chips)
+    deep = chips // wide
+    far = max(1, chips // 2 - 2)
 
     def kernel(
         times, y_hbm, n_hbm, w1_hbm, w2_hbm, tw_hbm, out_hbm, chg_ref,
         ent, ebf, xc, hid, grp, w1r, w2r, twr, w1s, w2s, temb, noise, res,
-        st, pb, cs, rx, tx, px, eo, ssq, load_sem, out_sem,
+        st, pb, cs, rx, tx, px, eo, ssq, load_sem, out_sem, near,
         halo_send, halo_recv, pair_send, pair_recv, cs_send, rx_recv, tx_send, px_recv,
         eo_send, ent_recv, ssq_send, ssq_recv,
     ):
@@ -67,6 +70,8 @@
         space = lax.axis_index("space")
         chip = step // 2
         core = step - 2 * chip
+        chip_z = chip // wide
+        chip_y = chip - chip_z * wide
         other = 1 - core
         partner = 2 * chip + other
         anchor = step == 0
@@ -93,21 +98,39 @@
 
         barrier = pltpu.get_barrier_semaphore()
 
-        @pl.loop(1, chips)
-        def _(d):
-            target = lax.rem(chip + d, chips)
-            pl.semaphore_signal(
-                barrier, inc=1, device_id={"step": 2 * target + core}, device_id_type=MESH
-            )
-
-        pl.semaphore_signal(barrier, inc=1, device_id={"step": partner}, device_id_type=MESH)
+        def signal(sem, **place):
+            pl.semaphore_signal(sem, inc=1, device_id=place, device_id_type=MESH)
+
+        def along_z(d):
+            return 2 * (lax.rem(chip_z + d + deep, deep) * wide + chip_y) + core
+
+        def along_y(d):
+            return 2 * (chip_z * wide + lax.rem(chip_y + d, wide)) + core
+
         for d in range(1, columns_of_space):
-            pl.semaphore_signal(
-                barrier,
-                inc=1,
-                device_id={"space": lax.rem(space + d, columns_of_space)},
-                device_id_type=MESH,
-            )
+            signal(barrier, space=lax.rem(space + d, columns_of_space))
+        signal(barrier, step=partner)
+        for d in range(1, wide):
+            signal(barrier, step=along_y(d))
+        close = columns_of_space + wide - 1
+        if deep > 1:
+            signal(barrier, step=along_z(1))
+            signal(barrier, step=along_z(-1))
+            close += 2
+
+        def greet(n):
+            if n < 2 and deep > 1:
+                signal(near.at[n], step=along_z(n + 1))
+                signal(near.at[n], step=along_z(-n - 1))
+            if n == 2:
+                for d in range(1, wide):
+                    signal(near.at[n], step=along_y(d))
+
+        def greeted(n):
+            if n < 2 and deep > 1:
+                pl.semaphore_wait(near.at[n], 2)
+            if n == 2:
+                pl.semaphore_wait(near.at[n], wide - 1)
 
         lane = lax.broadcasted_iota(jnp.int32, (1, EXT), 1)
         column = lax.rem(lane + (4 * COLS - OWN % COLS), COLS)
@@ -204,15 +227,17 @@
             weights = w2s[:, HID * first : HID * (first + high - low)]
             for n in range(0, NQ, CHUNK):
                 m = min(n + CHUNK, NQ)
-                grp[:, n:m] = jnp.dot(
+                grp[f % 2, :, n:m] = jnp.dot(
                     weights, hid[low * HID : high * HID, n:m], preferred_element_type=F32
                 )
+
+        def combine(f):
             masks = (not_last[:, Q0 : Q0 + NQ], None, not_first[:, Q0 : Q0 + NQ])
             total = None
             for b in range(3):
                 for c in range(3):
                     tap = b * 3 + c
-                    value = grp[tap * C : (tap + 1) * C, :]
+                    value = grp[f % 2, tap * C : (tap + 1) * C, :]
                     if masks[c] is not None:
                         value = jnp.where(masks[c], value, 0.0)
                     start = OWN - Q0 + COLS * (b - 1) + (c - 1)
@@ -232,7 +257,7 @@
 
         def drift(s, f):
             latent = ent[s, f]
-            value = decay_gain * latent + noise_gain * conv_two(f) + spread_gain * noise[f]
+            value = decay_gain * latent + noise_gain * combine(f) + spread_gain * noise[f]
             st[s, f] = value + jnp.where(anchor, latent, 0.0)
             pair_copy(s, f).start()
 
@@ -245,21 +270,17 @@
             for k in range(parts):
                 low, high, base = span(f, k)
 
-                @pl.loop(low, high)
-                def _(g):
-                    owner = g + base
-                    owner = jnp.where(owner >= chips, owner - chips, owner)
-
-                    @pl.when(owner != chip)
-                    def _():
-                        pltpu.make_async_remote_copy(
-                            src_ref=cs.at[s, f, g],
-                            dst_ref=rx.at[s, f, k, chip],
-                            send_sem=cs_send.at[s, f, k],
-                            recv_sem=rx_recv.at[s, f, k],
-                            device_id={"step": 2 * owner + core},
-                            device_id_type=MESH,
-                        ).start()
+                for g in range(low, high):
+                    owner = (g + base) % chips
+                    own_tile = chip == owner
+                    pltpu.make_async_remote_copy(
+                        src_ref=cs.at[s, f, g],
+                        dst_ref=rx.at[s, f, k, jnp.where(own_tile, chips, chip)],
+                        send_sem=cs_send.at[s, f, k],
+                        recv_sem=rx_recv.at[s, f, k],
+                        device_id={"step": jnp.where(own_tile, partner, 2 * owner + core)},
+                        device_id_type=MESH,
+                    ).start()
 
                 def keep(g):
                     rx[s, f, k, chip] = cs[s, f, g]
@@ -270,16 +291,16 @@
             for k in range(parts):
 
                 def work(g):
-                    given = rx.at[s, f, k, pl.ds(0, chips - 1)]
+                    given = rx.at[s, f, k, pl.ds(0, chips)]
                     pltpu.make_async_copy(given, given, rx_recv.at[s, f, k]).wait()
                     running = jnp.zeros((8, 128), F32)
                     for q in range(chips):
                         tx[s, f, k, q] = running
                         running = running + rx[s, f, k, q]
 
-                    @pl.loop(1, chips)
+                    @pl.loop(far, far + chips - 1)
                     def _(d):
-                        target = chip + d
+                        target = chip + jnp.where(d >= chips, d - chips + 1, d)
                         target = jnp.where(target >= chips, target - chips, target)
                         pltpu.make_async_remote_copy(
                             src_ref=tx.at[s, f, k, target],
@@ -320,8 +341,10 @@
                 if_mine(f, k, wait(high - low - 1), wait(high - low))
 
         def scan_done(s, f):
-            tiles_wait(cs, cs_send, s, f)
             for k in range(parts):
+                low, high, _ = span(f, k)
+                tiles = cs.at[s, f, pl.ds(low, high - low)]
+                pltpu.make_async_copy(tiles, tiles, cs_send.at[s, f, k]).wait()
 
                 def wait(g):
                     sent = tx.at[s, f, k, pl.ds(0, chips - 1)]
@@ -369,6 +392,16 @@
             ebf[s, f, :, OWN : OWN + PX] = ent[s, f].astype(BF)
             halo_start(s, f)
 
+        for copy in loads[:FRAMES]:
+            copy.wait()
+        for f in range(FRAMES):
+            ebf[0, f, :, OWN : OWN + PX] = ent[0, f].astype(BF)
+
+        pl.semaphore_wait(barrier, close)
+        greet(0)
+        for f in range(FRAMES):
+            halo_start(0, f)
+
         before = jnp.full((8, 128), times[0, 0], jnp.int32).astype(F32)
         after = jnp.full((8, 128), times[0, 1], jnp.int32).astype(F32)
         decay_gain, noise_gain, spread_gain = [
@@ -380,10 +413,6 @@
         frequency = jnp.exp(-math.log(10000.0) * place / (C // 2))
         angles = before[0:1, :] * frequency
         features = jnp.where(sine, jnp.sin(angles), jnp.cos(angles))
-        for copy in loads[:FRAMES]:
-            copy.wait()
-        for f in range(FRAMES):
-            ebf[0, f, :, OWN : OWN + PX] = ent[0, f].astype(BF)
         late[0].wait()
         for n in range(0, HID, 128):
             row = jnp.sum(twr[:, n : n + 128] * features, axis=0, keepdims=True)
@@ -401,29 +430,37 @@
         for copy in loads[FRAMES:]:
             copy.wait()
 
-        pl.semaphore_wait(barrier, chips + columns_of_space - 1)
-        for f in range(FRAMES):
-            halo_start(0, f)
-
         def out_copy(f):
             return pltpu.make_async_copy(res.at[f], out_hbm.at[:, f, :], out_sem.at[f])
 
         for s in range(2):
             im2col(s, 0)
             im2col(s, 1)
+            if s == 0:
+                greeted(0)
+                greet(1)
             conv_one(0)
             im2col(s, 2)
+            if s == 0:
+                greeted(1)
+                greet(2)
             conv_one(1)
+            conv_two(0)
             drift(s, 0)
             im2col(s, 3)
             conv_one(2)
+            if s == 0:
+                greeted(2)
             chip_sum(s, 0)
+            conv_two(1)
+            conv_one(3)
             drift(s, 1)
-            conv_one(3)
+            conv_two(2)
+            conv_two(3)
+            drift(s, 2)
             chip_sum(s, 1)
-            drift(s, 2)
+            drift(s, 3)
             chip_sum(s, 2)
-            drift(s, 3)
             chip_sum(s, 3)
             for f in range(FRAMES):
                 own(s, f)
@@ -491,7 +528,7 @@
         pltpu.VMEM((2, FRAMES, C, EXT), BF),
         pltpu.VMEM((FRAMES * 9 * C, NQ), BF),
         pltpu.VMEM((FRAMES * HID, NQ), BF),
-        pltpu.VMEM((9 * C, NQ), F32),
+        pltpu.VMEM((2, 9 * C, NQ), F32),
         pltpu.VMEM((27 * C, HID), BF),
         pltpu.VMEM((3, C, 9 * HID), BF),
         pltpu.VMEM((C, HID), F32),
@@ -503,13 +540,14 @@
         pltpu.VMEM((2, FRAMES, C, PX), F32),
         pltpu.VMEM((2, FRAMES, HALF, PX), F32),
         pltpu.VMEM((2, FRAMES, TILES, 8, 128), F32),
-        pltpu.VMEM((2, FRAMES, parts, chips, 8, 128), F32),
+        pltpu.VMEM((2, FRAMES, parts, chips + 1, 8, 128), F32),
         pltpu.VMEM((2, FRAMES, parts, chips, 8, 128), F32),
         pltpu.VMEM((2, FRAMES, TILES, 8, 128), F32),
         pltpu.VMEM((2, FRAMES, HALF, PX), F32),
         pltpu.VMEM((columns_of_space + 1, 8, 128), F32),
         pltpu.SemaphoreType.DMA((2 * FRAMES + 3,)),
         pltpu.SemaphoreType.DMA((FRAMES,)),
+        pltpu.SemaphoreType.REGULAR((3,)),
         pltpu.SemaphoreType.DMA((2, FRAMES, 2)),
         pltpu.SemaphoreType.DMA((2, FRAMES, 2)),
         pltpu.SemaphoreType.DMA((2, FRAMES)),

time: 80.5 us -> 78.2 us (0.971)
  Pallas kernels: 76 us -> 73.7 us
    pallas_call x1, Pallas kernels: 76 us -> 73.7 us  [local(): pl.pallas_call(kernel, out_shape=(jax.ShapeDtypeStruct((C, FRAMES, PX), F...]
where the time goes in v3:
time: 78.2 us; the launch traced here: 78.1 us
  Pallas kernels  73.7 us (94%)
  between operations  2.39 us (3%)
  local copies, waits for them, and re-layouts  1.98 us (3%)
    pallas_call x1, Pallas kernels, local(): pl.pallas_call(kernel, out_shape=(jax.ShapeDtypeStruct((C, FRAMES, PX), F...  73.7 us
    unnamed x1, local copies, waits for them, and re-layouts  1.98 us

profile of v3, /device:TPU:1, one launch (start us, length us, event | category | flops | bytes accessed | tf_op | source)
XLA Modules:
  0.0 78.1 jit_solution(18146393626792472658)
XLA Ops:
  0.6 73.7 %shard_map.77 = (f32[64,4,640]{2,1,0:T(4,128)}, f32[1]{0:T(128)}) custom-call(s32[1,2]{1,0:T(1,128)} %times.1, f32[64,4,640]{2,1,0:T(4,128)} %bitcast.8, f32[64,4,640]{2,1,0:T(4,128)} %bitcast.9, bf16[1728,256]{1,0:T(8,128)(2,1)} %bitcast.6, bf16[3,64,2304]{2,1,0:T(8,128)(2,1)} %w2_hbm.1, f32[64,256]{1,0:T(8,128)} %tw_hbm.1), custom_call_target="tpu_custom_call" | custom-call | tf_op jit(solution)/shard_map/pallas_call | solution.py:576
  74.3 2.0 %copy.10 = f32[1,64,4,640]{3,2,1,0:T(4,128)} copy(f32[1,64,4,640]{3,2,1,0:T(4,128)} %bitcast.7) | data formatting | bytes 1310720

commit v4 on v3

--- a/solution.py
+++ b/solution.py
@@ -62,9 +62,9 @@
     def kernel(
         times, y_hbm, n_hbm, w1_hbm, w2_hbm, tw_hbm, out_hbm, chg_ref,
         ent, ebf, xc, hid, grp, w1r, w2r, twr, w1s, w2s, temb, noise, res,
-        st, pb, cs, rx, tx, px, eo, ssq, load_sem, out_sem, near,
+        st, pb, cs, rx, tx, px, eo, eob, ssq, red, load_sem, out_sem, near,
         halo_send, halo_recv, pair_send, pair_recv, cs_send, rx_recv, tx_send, px_recv,
-        eo_send, ent_recv, ssq_send, ssq_recv,
+        eo_send, ent_recv, half_send, red_send, red_recv,
     ):
         step = lax.axis_index("step")
         space = lax.axis_index("space")
@@ -156,16 +156,48 @@
             )
             return right, left
 
+        def half_copies(f):
+            ahead = lax.rem(space + 1, columns_of_space)
+            behind = lax.rem(space + columns_of_space - 1, columns_of_space)
+            pairs = []
+            for n, (place, start, landing) in enumerate(
+                ((ahead, PX - 256, 0), (behind, 0, OWN + PX))
+            ):
+                landed = ebf.at[1, f, mine_rows, pl.ds(landing, 256)]
+                own_edge = pltpu.make_async_remote_copy(
+                    src_ref=ebf.at[1, f, mine_rows, pl.ds(OWN + start, 256)],
+                    dst_ref=landed,
+                    send_sem=halo_send.at[1, f, n],
+                    recv_sem=halo_recv.at[1, f, n],
+                    device_id={"space": place},
+                    device_id_type=MESH,
+                )
+                other_edge = pltpu.make_async_remote_copy(
+                    src_ref=eob.at[f, :, pl.ds(start, 256)],
+                    dst_ref=landed,
+                    send_sem=half_send.at[f, n],
+                    recv_sem=halo_recv.at[1, f, n],
+                    device_id={"space": place, "step": partner},
+                    device_id_type=MESH,
+                )
+                pairs.append((own_edge, other_edge))
+            return pairs
+
+        def halo_sends(s, f):
+            return half_copies(f) if s == 1 else [(copy,) for copy in halo_copies(s, f)]
+
         def halo_start(s, f):
-            right, left = halo_copies(s, f)
+            right, left = halo_sends(s, f)
 
             @pl.when(space < columns_of_space - 1)
             def _():
-                right.start()
+                for copy in right:
+                    copy.start()
 
             @pl.when(space > 0)
             def _():
-                left.start()
+                for copy in left:
+                    copy.start()
 
         def halo_wait(s, f):
             right, left = halo_copies(s, f)
@@ -179,19 +211,23 @@
                 left.wait_recv()
 
         def halo_done(s, f):
-            right, left = halo_copies(s, f)
+            right, left = halo_sends(s, f)
 
             @pl.when(space < columns_of_space - 1)
             def _():
-                right.wait_send()
+                for copy in right:
+                    copy.wait_send()
 
             @pl.when(space > 0)
             def _():
-                left.wait_send()
+                for copy in left:
+                    copy.wait_send()
 
         def im2col(s, f):
             halo_wait(s, f)
             whole = ebf[s, f]
+            if s == 1:
+                whole = jnp.where(anchor, ebf[0, f], whole)
             zero = jnp.zeros_like(whole)
             shifted = (jnp.where(not_last, whole, zero), whole, jnp.where(not_first, whole, zero))
             for b in range(3):
@@ -375,22 +411,58 @@
             )
             first = jnp.where(core == 0, st[s, f, mine_rows, :], pb[s, f])
             after = before + first
-            eo[s, f] = jnp.where(core == 0, after, before)
+            own_part = jnp.where(core == 0, before, after)
+            other_part = jnp.where(core == 0, after, before)
+            eo[s, f] = other_part
             enter_copy(s, f).start()
-            ent[s + 1, f, mine_rows, :] = jnp.where(core == 0, before, after)
+            ent[s + 1, f, mine_rows, :] = own_part
+            if s == 0:
+                ebf[1, f, mine_rows, OWN : OWN + PX] = own_part.astype(BF)
+                eob[f] = other_part.astype(BF)
+                halo_start(1, f)
+                return None
+            first_step = chip == 0
+            squares = []
+            for keep_from, now, was, now_step, was_step in (
+                (anchor, own_part, ent[1, f, mine_rows, :], st[1, f, mine_rows, :], st[0, f, mine_rows, :]),
+                (first_step & (core == 1), other_part, eo[0, f], pb[1, f], pb[0, f]),
+            ):
+                keep = jnp.where(keep_from, 0.0, 1.0)
+                change = (keep * now + now_step) - (keep * was + was_step)
+                change = change * change
+                square = None
+                for r in range(HALF // 8):
+                    for b in range(BLOCKS):
+                        part = change[8 * r : 8 * r + 8, 128 * b : 128 * b + 128]
+                        square = part if square is None else square + part
+                squares.append(square)
+            return squares
 
         def entered(s, f):
-            pltpu.make_async_copy(
-                ent.at[s + 1, f, other_rows, :], ent.at[s + 1, f, other_rows, :], ent_recv.at[s, f]
-            ).wait()
+            theirs = ent.at[s + 1, f, other_rows, :]
+            pltpu.make_async_copy(theirs, theirs, ent_recv.at[s, f]).wait()
+            if s == 0:
+                ebf[1, f, other_rows, OWN : OWN + PX] = ent[1, f, other_rows, :].astype(BF)
 
             @pl.when(anchor)
             def _():
                 ent[s + 1, f] = ent[0, f]
 
-        def latent_out(s, f):
-            ebf[s, f, :, OWN : OWN + PX] = ent[s, f].astype(BF)
-            halo_start(s, f)
+        def sum_copy(n, d):
+            place = {"space": lax.rem(space + d, columns_of_space)}
+            if n == 1:
+                place["step"] = partner
+            return pltpu.make_async_remote_copy(
+                src_ref=ssq.at[n],
+                dst_ref=red.at[core, space],
+                send_sem=red_send.at[n, d],
+                recv_sem=red_recv.at[core, space],
+                device_id=place,
+                device_id_type=MESH,
+            )
+
+        sums = [(0, d) for d in range(1, columns_of_space)]
+        sums += [(1, d) for d in range(columns_of_space)]
 
         for copy in loads[:FRAMES]:
             copy.wait()
@@ -464,40 +536,20 @@
             chip_sum(s, 3)
             for f in range(FRAMES):
                 own(s, f)
-            square = None
-            enter(s, 0)
+            squares = [enter(s, 0)]
             for f in range(FRAMES):
                 if f + 1 < FRAMES:
-                    enter(s, f + 1)
+                    squares.append(enter(s, f + 1))
+                if s == 1 and f + 2 == FRAMES:
+                    for n in range(2):
+                        ssq[n] = squares[0][n] + squares[1][n] + squares[2][n] + squares[3][n]
+                    red[core, space] = ssq[0]
+                    for n, d in sums:
+                        sum_copy(n, d).start()
                 entered(s, f)
-                if s == 0:
-                    latent_out(1, f)
-                else:
-                    keep = jnp.where(anchor, 0.0, 1.0)
-                    reached = keep * ent[2, f] + st[1, f]
-                    change = reached - (keep * ent[1, f] + st[0, f])
-                    change = change * change
-                    for r in range(C // 8):
-                        for b in range(BLOCKS):
-                            part = change[8 * r : 8 * r + 8, 128 * b : 128 * b + 128]
-                            square = part if square is None else square + part
-                    res[f] = reached
+                if s == 1:
+                    res[f] = jnp.where(anchor, 0.0, 1.0) * ent[2, f] + st[1, f]
                     out_copy(f).start()
-            if s == 1:
-                ssq[0] = square
-
-        def ssq_copy(d):
-            return pltpu.make_async_remote_copy(
-                src_ref=ssq.at[0],
-                dst_ref=ssq.at[columns_of_space + 1 - d],
-                send_sem=ssq_send.at[d - 1],
-                recv_sem=ssq_recv.at[columns_of_space - 1 - d],
-                device_id={"space": lax.rem(space + d, columns_of_space)},
-                device_id_type=MESH,
-            )
-
-        for d in range(1, columns_of_space):
-            ssq_copy(d).start()
 
         for s in range(2):
             for f in range(FRAMES):
@@ -508,18 +560,16 @@
         for f in range(FRAMES):
             out_copy(f).wait()
 
-        for d in range(1, columns_of_space):
-            ssq_copy(d).wait_send()
-        for d in range(1, columns_of_space):
-            ssq_copy(columns_of_space - d).wait_recv()
+        for n, d in sums:
+            sum_copy(n, d).wait_send()
+        for n, d in sums:
+            given = (core if n == 0 else other, lax.rem(space + d, columns_of_space))
+            cells = red.at[given]
+            pltpu.make_async_copy(cells, cells, red_recv.at[given]).wait()
         total = None
-        for x in range(columns_of_space):
-            part = None
-            for d in range(columns_of_space):
-                place = 0 if d == 0 else d + 1
-                term = jnp.where(lax.rem(space + d, columns_of_space) == x, ssq[place], 0.0)
-                part = term if part is None else part + term
-            total = part if total is None else total + part
+        for n in range(2):
+            for x in range(columns_of_space):
+                total = red[n, x] if total is None else total + red[n, x]
         mean = jnp.full((8, 128), jnp.sum(total), F32) / cell_count
         chg_ref[0] = jnp.max(jnp.sqrt(mean))
 
@@ -544,7 +594,9 @@
         pltpu.VMEM((2, FRAMES, parts, chips, 8, 128), F32),
         pltpu.VMEM((2, FRAMES, TILES, 8, 128), F32),
         pltpu.VMEM((2, FRAMES, HALF, PX), F32),
-        pltpu.VMEM((columns_of_space + 1, 8, 128), F32),
+        pltpu.VMEM((FRAMES, HALF, PX), BF),
+        pltpu.VMEM((2, 8, 128), F32),
+        pltpu.VMEM((2, columns_of_space, 8, 128), F32),
         pltpu.SemaphoreType.DMA((2 * FRAMES + 3,)),
         pltpu.SemaphoreType.DMA((FRAMES,)),
         pltpu.SemaphoreType.REGULAR((3,)),
@@ -558,8 +610,9 @@
         pltpu.SemaphoreType.DMA((2, FRAMES, parts)),
         pltpu.SemaphoreType.DMA((2, FRAMES)),
         pltpu.SemaphoreType.DMA((2, FRAMES)),
-        pltpu.SemaphoreType.DMA((columns_of_space,)),
-        pltpu.SemaphoreType.DMA((columns_of_space,)),
+        pltpu.SemaphoreType.DMA((FRAMES, 2)),
+        pltpu.SemaphoreType.DMA((2, columns_of_space)),
+        pltpu.SemaphoreType.DMA((2, columns_of_space)),
     ]
     return kernel, scratch
 

time: 78.2 us -> 77.2 us (0.987)
  Pallas kernels: 73.7 us -> 72.7 us
    pallas_call x1, Pallas kernels: 73.7 us -> 72.7 us  [local(): pl.pallas_call(kernel, out_shape=(jax.ShapeDtypeStruct((C, FRAMES, PX), F...]
where the time goes in v4:
time: 77.2 us; the launch traced here: 77 us
  Pallas kernels  72.7 us (94%)
  between operations  2.39 us (3%)
  local copies, waits for them, and re-layouts  1.98 us (3%)
    pallas_call x1, Pallas kernels, local(): pl.pallas_call(kernel, out_shape=(jax.ShapeDtypeStruct((C, FRAMES, PX), F...  72.7 us
    unnamed x1, local copies, waits for them, and re-layouts  1.98 us

profile of v4, /device:TPU:1, one launch (start us, length us, event | category | flops | bytes accessed | tf_op | source)
XLA Modules:
  0.0 77.0 jit_solution(12608173696612320378)
XLA Ops:
  0.6 72.7 %shard_map.77 = (f32[64,4,640]{2,1,0:T(4,128)}, f32[1]{0:T(128)}) custom-call(s32[1,2]{1,0:T(1,128)} %times.1, f32[64,4,640]{2,1,0:T(4,128)} %bitcast.8, f32[64,4,640]{2,1,0:T(4,128)} %bitcast.9, bf16[1728,256]{1,0:T(8,128)(2,1)} %bitcast.6, bf16[3,64,2304]{2,1,0:T(8,128)(2,1)} %w2_hbm.1, f32[64,256]{1,0:T(8,128)} %tw_hbm.1), custom_call_target="tpu_custom_call" | custom-call | tf_op jit(solution)/shard_map/pallas_call | solution.py:629
  73.3 2.0 %copy.10 = f32[1,64,4,640]{3,2,1,0:T(4,128)} copy(f32[1,64,4,640]{3,2,1,0:T(4,128)} %bitcast.7) | data formatting | bytes 1310720

commit v5 on v4

--- a/solution.py
+++ b/solution.py
@@ -88,7 +88,7 @@
             pltpu.make_async_copy(w1_hbm, w1r, load_sem.at[2 * FRAMES + 1]),
             pltpu.make_async_copy(w2_hbm, w2r, load_sem.at[2 * FRAMES + 2]),
         ]
-        for copy in loads[:FRAMES] + late + loads[FRAMES:]:
+        for copy in loads[:FRAMES] + late:
             copy.start()
 
         for s in range(2):
@@ -473,6 +473,8 @@
         greet(0)
         for f in range(FRAMES):
             halo_start(0, f)
+        for copy in loads[FRAMES:]:
+            copy.start()
 
         before = jnp.full((8, 128), times[0, 0], jnp.int32).astype(F32)
         after = jnp.full((8, 128), times[0, 1], jnp.int32).astype(F32)
@@ -499,8 +501,6 @@
                 w2s[tap * C : (tap + 1) * C, a * HID : (a + 1) * HID] = w2r[
                     a, :, tap * HID : (tap + 1) * HID
                 ]
-        for copy in loads[FRAMES:]:
-            copy.wait()
 
         def out_copy(f):
             return pltpu.make_async_copy(res.at[f], out_hbm.at[:, f, :], out_sem.at[f])
@@ -518,6 +518,9 @@
                 greet(2)
             conv_one(1)
             conv_two(0)
+            if s == 0:
+                for copy in loads[FRAMES:]:
+                    copy.wait()
             drift(s, 0)
             im2col(s, 3)
             conv_one(2)

time: 77.2 us -> 77.5 us (level)
  no operation moved by 1% of the time
where the time goes in v5:
time: 77.5 us; the launch traced here: 77.3 us
  Pallas kernels  72.9 us (94%)
  between operations  2.39 us (3%)
  local copies, waits for them, and re-layouts  1.98 us (3%)
    pallas_call x1, Pallas kernels, local(): pl.pallas_call(kernel, out_shape=(jax.ShapeDtypeStruct((C, FRAMES, PX), F...  72.9 us
    unnamed x1, local copies, waits for them, and re-layouts  1.98 us

profile of v5, /device:TPU:1, one launch (start us, length us, event | category | flops | bytes accessed | tf_op | source)
XLA Modules:
  0.0 77.3 jit_solution(3356292153973504850)
XLA Ops:
  0.6 72.9 %shard_map.77 = (f32[64,4,640]{2,1,0:T(4,128)}, f32[1]{0:T(128)}) custom-call(s32[1,2]{1,0:T(1,128)} %times.1, f32[64,4,640]{2,1,0:T(4,128)} %bitcast.8, f32[64,4,640]{2,1,0:T(4,128)} %bitcast.9, bf16[1728,256]{1,0:T(8,128)(2,1)} %bitcast.6, bf16[3,64,2304]{2,1,0:T(8,128)(2,1)} %w2_hbm.1, f32[64,256]{1,0:T(8,128)} %tw_hbm.1), custom_call_target="tpu_custom_call" | custom-call | tf_op jit(solution)/shard_map/pallas_call | solution.py:632
  73.6 2.0 %copy.10 = f32[1,64,4,640]{3,2,1,0:T(4,128)} copy(f32[1,64,4,640]{3,2,1,0:T(4,128)} %bitcast.7) | data formatting | bytes 1310720
